TPU v7x, 128 devices: a whole 4x4x4 slice. The times are simulated.
128 devices in a mesh: refl: 4 (over y_hi, core), atom: 32 (over z, x, y_lo).
Axes of the slice: x: 4, y: 4 (y_hi: 2, y_lo: 2; y = y_hi * 2 + y_lo), z: 4, core: 2. Of those that a mesh axis runs over, the one named last changes fastest.
Arguments:
- features: bfloat16 [65536, 128], P('atom'), may hold values from -6 to 6
- ln_gain: float32 [2, 128], replicated, may hold values from 0.25 to 1.75
- w_qkv: bfloat16 [2, 3, 128, 128], P(None, None, None, 'refl'), may hold values from -0.5 to 0.5
- w_out: bfloat16 [2, 128, 128], replicated, may hold values from -0.5 to 0.5
- w_coord: bfloat16 [3, 128], replicated, may hold values from -0.5 to 0.5
- noisy_coords: float32 [3, 65536], P(None, 'atom'), may hold values from 0 to 1
- scatter_power: float32 [65536], P('atom'), may hold values from 0.5 to 4
- route: int32 [32, 32], P('atom'), may hold values from 0 to 31, each once within a row
- miller: int32 [3, 4096], P(None, 'refl'), may hold values from -12 to 12
- rotations: int32 [4, 3, 3], replicated, may hold values from -1 to 1, as said below
- shifts: float32 [4, 3], replicated, may hold values from 0 to 1
- observed: float32 [4096], P('refl'), may hold values from 0.3 to 3
- obs_weight: float32 [4096], P('refl'), may hold values from 0.2 to 2
Outputs:
- atom_out: bfloat16 [65536, 128], P('atom')
- amplitude: float32 [4096], P(('refl', 'atom'))
- coord_grad: float32 [3, 65536], P(None, 'atom')
Inputs may be any that keep to these rules, and one draw needn't show every extreme that they name: Each row of route names every block of a shard once. `rotations`: each of the 4 matrices is a permutation matrix with signs.
All inputs are finite; a program needn't handle non-finite values.
Results may differ from a plain program's by a relative error of at most 0.012.
Values may be sent and summed in bfloat16 or wider, within the bound.
No kernel may reach another device: no remote copies, remote signals or barrier semaphores. Data moves between devices by JAX's collectives and lax.ppermute only.
A program may use at most 64 MiB of HBM per device.

v0:
```python
import math

import jax
import jax.numpy as jnp
from jax import lax
from jax.sharding import PartitionSpec as P

HEAD_FEATURES = 32
QWIN = 32
WINDOW_KEYS = 128
LAYERS = 2


def padded_2(cells, sides, width):
    for axis, dim in sides:
        count = lax.axis_size(axis)
        ends = count - 1
        head = lax.slice_in_dim(cells, 0, width, axis=dim)
        tail = lax.slice_in_dim(cells, cells.shape[dim] - width, cells.shape[dim], axis=dim)
        cells = jnp.concatenate(
            [
                lax.ppermute(tail, axis, [(i, (i + 1) % count) for i in range(ends)]),
                cells,
                lax.ppermute(head, axis, [((i + 1) % count, i) for i in range(ends)]),
            ],
            axis=dim,
        )
    return cells


def layer_norm(x, gain):
    mean = jnp.mean(x, axis=-1, keepdims=True)
    cent = x - mean
    var = jnp.mean(cent * cent, axis=-1, keepdims=True)
    return (cent * lax.rsqrt(var + 1e-05) * gain).astype(jnp.bfloat16)


def window_blocks(padded, window_count):
    parts = [
        padded[QWIN * j : QWIN * j + window_count * QWIN].reshape(window_count, QWIN, -1)
        for j in range(WINDOW_KEYS // QWIN)
    ]
    return jnp.concatenate(parts, axis=1)


def attend_windowed(query_rows, padded_keys, padded_values, valid_mask):
    window_count = query_rows.shape[0] // QWIN
    head_count = query_rows.shape[1] // HEAD_FEATURES
    qwin = query_rows.reshape(window_count, QWIN, head_count, HEAD_FEATURES)
    kwin = window_blocks(padded_keys, window_count).reshape(
        window_count, WINDOW_KEYS, head_count, HEAD_FEATURES
    )
    window_values = window_blocks(padded_values, window_count).reshape(
        window_count, WINDOW_KEYS, head_count, HEAD_FEATURES
    )
    mwin = window_blocks(valid_mask, window_count)[..., 0]
    scores = jnp.einsum(
        "wqhd,wkhd->whqk", qwin, kwin, preferred_element_type=jnp.float32
    ) * HEAD_FEATURES ** (-0.5)
    scores = jnp.where(mwin[:, None, None, :] > 0.5, scores, -1e30)
    top = jnp.max(scores, axis=-1, keepdims=True)
    expo = jnp.exp(scores - top)
    probs = (expo / jnp.sum(expo, axis=-1, keepdims=True)).astype(jnp.bfloat16)
    out = jnp.einsum("whqk,wkhd->wqhd", probs, window_values, preferred_element_type=jnp.float32)
    return out.reshape(window_count * QWIN, head_count * HEAD_FEATURES).astype(jnp.bfloat16)


def phases(hs_blk, tsh_blk, pos):
    turn = (
        hs_blk[:, 0, :, None] * pos[0]
        + hs_blk[:, 1, :, None] * pos[1]
        + hs_blk[:, 2, :, None] * pos[2]
    )
    angle = 2.0 * math.pi * (turn + tsh_blk[:, :, None])
    return (jnp.cos(angle), jnp.sin(angle))


def loss_terms(totals, observed, obs_weight, nrefl):
    amplitude = jnp.sqrt(totals[0] * totals[0] + totals[1] * totals[1] + 1.0)
    slope = 2.0 * obs_weight * (amplitude - observed) / (amplitude * math.sqrt(nrefl))
    return (amplitude, jnp.stack([slope * totals[0], slope * totals[1]]))


def neighbour_rows(keyval, window_border):
    return padded_2(keyval, (("atom", 0),), window_border)


def body(
    features,
    ln_gain,
    w_qkv,
    w_out,
    w_coord,
    noisy_coords,
    scatter_power,
    route,
    miller,
    rotations,
    shifts,
    observed,
    obs_weight,
):
    shards = lax.axis_size("atom")
    rank = lax.axis_index("atom")
    local = features.shape[0]
    natom = local * shards
    window_border = (WINDOW_KEYS - QWIN) // 2
    place = rank * local - window_border + jnp.arange(local + 2 * window_border, dtype=jnp.int32)
    valid_mask = ((place >= 0) & (place < natom)).astype(jnp.float32)[:, None]
    x = features.astype(jnp.float32)
    for layer in range(LAYERS):
        normed = layer_norm(x, ln_gain[layer])
        proj = jnp.einsum(
            "nc,jcd->jnd", normed, w_qkv[layer], preferred_element_type=jnp.float32
        ).astype(jnp.bfloat16)
        width = proj.shape[2]
        keyval = jnp.concatenate([proj[1], proj[2]], axis=1)
        padded = neighbour_rows(keyval, window_border)
        head_rows = attend_windowed(proj[0], padded[:, :width], padded[:, width:], valid_mask)
        out_weight = w_out[layer]
        x = x + jnp.dot(
            lax.all_gather(head_rows, "refl", axis=1, tiled=True),
            out_weight,
            preferred_element_type=jnp.float32,
        )
    atom_out = x.astype(jnp.bfloat16)
    moved = noisy_coords + 0.02 * jnp.dot(w_coord, atom_out.T, preferred_element_type=jnp.float32)
    packed = jnp.concatenate([moved, scatter_power[None, :]], axis=0)
    blk = local // shards
    packed = packed.reshape(4, shards, blk)[:, route[0], :]
    arrived = lax.all_to_all(packed, "atom", split_axis=1, concat_axis=1, tiled=True).reshape(
        4, local
    )
    pos = arrived[:3]
    power = arrived[3]
    group = miller.shape[1]
    nops = rotations.shape[0]
    nrefl = group * lax.axis_size("refl")
    hs = jnp.einsum(
        "skc,kr->scr",
        rotations.astype(jnp.float32),
        miller.astype(jnp.float32),
        precision=lax.Precision.HIGHEST,
    )
    tsh = jnp.einsum(
        "kr,sk->sr", miller.astype(jnp.float32), shifts, precision=lax.Precision.HIGHEST
    )
    norm = 1.0 / math.sqrt(nops * natom)
    rows = min(512, group)
    turns = group // rows
    hs_b = hs.reshape(nops, 3, turns, rows).transpose(2, 0, 1, 3)
    ts_b = tsh.reshape(nops, turns, rows).transpose(1, 0, 2)

    def structure(cosv, sinv):
        fa = jnp.einsum("sra,a->r", cosv, power, precision=lax.Precision.HIGHEST)
        fb = jnp.einsum("sra,a->r", sinv, power, precision=lax.Precision.HIGHEST)
        return jnp.stack([fa, fb]) * norm

    def forward(carry, item):
        cosv, sinv = phases(item[0], item[1], pos)
        return (carry, structure(cosv, sinv))

    unused, parts = lax.scan(forward, 0.0, (hs_b, ts_b))
    partial_sums = parts.transpose(1, 0, 2).reshape(2, group)
    share = group // shards
    totals = lax.psum(partial_sums, "atom")
    amp_all, slopes = loss_terms(totals, observed, obs_weight, nrefl)
    amplitude = lax.dynamic_slice_in_dim(amp_all, rank * share, share, 0)
    sl_b = slopes.reshape(2, turns, rows).transpose(1, 0, 2)
    factor = 2.0 * math.pi * norm

    def accumulate(total, hs_blk, cosv, sinv, slope_blk):
        coef = (
            factor
            * power
            * (cosv * slope_blk[1][None, :, None] - sinv * slope_blk[0][None, :, None])
        )
        return total + jnp.einsum("scr,sra->ca", hs_blk, coef, precision=lax.Precision.HIGHEST)

    empty = jnp.zeros((3, local), jnp.float32)

    def backward(total, item):
        cosv, sinv = phases(item[0], item[1], pos)
        return (accumulate(total, item[0], cosv, sinv, item[2]), None)

    local_grad, unused = lax.scan(backward, empty, (hs_b, ts_b, sl_b))
    coord_grad = lax.psum(local_grad, "refl")
    return (atom_out, amplitude, coord_grad)


def solution(mesh):
    placed = (
        P("atom", None),
        P(),
        P(None, None, None, "refl"),
        P(),
        P(),
        P(None, "atom"),
        P("atom"),
        P("atom", None),
        P(None, "refl"),
        P(),
        P(),
        P("refl"),
        P("refl"),
    )
    return jax.shard_map(
        body,
        mesh=mesh,
        in_specs=placed,
        out_specs=(P("atom", None), P(("refl", "atom")), P(None, "atom")),
        check_vma=False,
    )
```

profile of v0, /device:TPU:0, one launch (start us, length us, event | category | flops | bytes accessed | tf_op | source)
XLA Modules:
  0.0 506.5 jit_solution(986680239627520885)
XLA Ops:
  0.7 1.3 copy.101
  4.3 3.6 collective-permute-start
  7.9 1.3 collective-permute-start.1
  10.0 3.7 collective-permute-done.1
  22.8 1.2 copy.105
  25.5 3.2 fusion.139
  28.7 2.7 fusion.46
  32.1 8.4 %all_gather.6 = bf16[2048,128]{0,1:T(8,128)(2,1)S(1)} all-gather(bf16[2048,32]{0,1:T(8,128)(2,1)S(1)} %convert_element_type.85), channel_id=1, replica_groups=mesh['refl'=4,'atom'=32] {'refl'}, dimensions={1}, use_global_device_ids=true | all-gather | bytes 655360 | tf_op jit(solution)/shard_map/all_gather | solution.py:122
  41.6 3.9 collective-permute-start.2
  45.5 1.8 collective-permute-start.3
  48.2 2.9 collective-permute-done.3
  54.4 1.3 reshape.328
  56.9 1.3 reshape.329
  60.8 1.3 reshape.322
  63.3 1.3 reshape.323
  67.2 3.2 fusion.143
  70.4 2.9 fusion.47
  74.1 8.6 %all_gather.7 = bf16[2048,128]{0,1:T(8,128)(2,1)S(1)} all-gather(bf16[2048,32]{0,1:T(8,128)(2,1)S(1)} %convert_element_type.93), channel_id=1, replica_groups=mesh['refl'=4,'atom'=32] {'refl'}, dimensions={1}, use_global_device_ids=true | all-gather | bytes 655360 | tf_op jit(solution)/shard_map/all_gather | solution.py:122
  84.8 12.2 %all-to-all-start = ((f32[32,1,256]{2,1,0:T(1,128)}), f32[32,1,256]{2,1,0:T(1,128)S(1)}, u32[]{:S(2)}, u32[]{:S(2)}) async-start(f32[32,1,256]{2,1,0:T(1,128)} %reshape.358), calls=%async_computation | async-start | bytes 65536 | tf_op jit(solution)/shard_map/all_to_all | solution.py:131
  98.3 6.9 %all-to-all-done = f32[32,1,256]{2,1,0:T(1,128)S(1)} async-done(((f32[32,1,256]{2,1,0:T(1,128)}), f32[32,1,256]{2,1,0:T(1,128)S(1)}, u32[]{:S(2)}, u32[]{:S(2)}) %all-to-all-start) | async-done | bytes 32800 | tf_op jit(solution)/shard_map/all_to_all | solution.py:131
  106.8 155.7 %while.21 = (s32[]{:T(128)}, f32[2,2,512]{2,1,0:T(2,128)S(1)}, f32[2,4,3,512]{3,1,2,0:T(4,128)S(1)}, f32[3,2048]{1,0:T(4,128)S(1)}, f32[2,4,512]{2,1,0:T(4,128)S(1)}, /*index=5*/f32[2048]{0:T(1024)S(1)}, s32[]{:T(128)}) while((s32[]{:T(128)}, f32[2,2,512]{2,1,0:T(2,128)S(1)}, f32[2,4,3,512]{3,1,2,0:T(4,128)S(1)}, f32[3,2048]{1,0:T(4,128)S(1)}, ...), condition=%wide.region_11.12_spmd, body=%wide.region_8.11_spmd.sunk | while | flops 60819456 | bytes 33804404 | solution.py:163
  106.9 70.5 %cosine_reduce_fusion.2 = (f32[512,2048]{1,0:T(8,128)}, f32[512,2048]{1,0:T(8,128)S(1)}) fusion(f32[4,512]{1,0:T(4,128)S(1)} %dynamic-slice_bitcast_fusion.8, f32[2048]{0:T(1024)S(1)} %bitcast.254, f32[4,512]{1,0:T(4,128)S(1)} %get-tuple-element.305, f32[2048]{0:T(1024)S(1)} %bitcast.255, f32[4,512]{1,0:T(4,128)S(1)} %get-tuple-element.307, ...), kind=kLoop, calls=%fused_computation.2.clone.1 | loop fusion | flops 35651584 | bytes 8445952 | tf_op jit(solution)/shard_map/while/body/eval_jaxpr/sra,a->r/reduce_sum | solution.py:155
  177.4 3.6 convolution_bitcast_fusion.4
  181.0 3.6 convolution_bitcast_fusion.5
  184.8 70.5 %cosine_reduce_fusion.2 = (f32[512,2048]{1,0:T(8,128)}, f32[512,2048]{1,0:T(8,128)S(1)}) fusion(f32[4,512]{1,0:T(4,128)S(1)} %dynamic-slice_bitcast_fusion.8, f32[2048]{0:T(1024)S(1)} %bitcast.254, f32[4,512]{1,0:T(4,128)S(1)} %get-tuple-element.305, f32[2048]{0:T(1024)S(1)} %bitcast.255, f32[4,512]{1,0:T(4,128)S(1)} %get-tuple-element.307, ...), kind=kLoop, calls=%fused_computation.2.clone.1 | loop fusion | flops 35651584 | bytes 8445952 | tf_op jit(solution)/shard_map/while/body/eval_jaxpr/sra,a->r/reduce_sum | solution.py:155
  255.2 3.6 convolution_bitcast_fusion.4
  258.9 3.6 convolution_bitcast_fusion.5
  262.5 80.0 %psum.14 = f32[2,1024]{1,0:T(2,128)S(1)} all-reduce(f32[2,1024]{1,0:T(2,128)S(1)} %bitcast.264), channel_id=1, replica_groups=mesh['refl'=4,'atom'=32] {'atom'}, use_global_device_ids=true, to_apply=%region_12.13 | all-reduce | flops 2048 | bytes 16384 | tf_op jit(solution)/shard_map/psum | solution.py:166
  342.6 149.2 %while.22 = (s32[]{:T(128)}, f32[3,2048]{1,0:T(4,128)S(1)}, f32[2,4,3,512]{3,2,1,0:T(4,128)S(1)}, f32[2048]{0:T(1024)S(1)}, f32[3,2048]{1,0:T(4,128)S(1)}, /*ind...) while((s32[]{:T(128)}, f32[3,2048]{1,0:T(4,128)S(1)}, ...), condition=%wide.region_14.15_spmd.clone, body=%wide.region_13.14_spmd.clone.sunk | while | flops 197146624 | bytes 381067 | solution.py:186
  342.8 74.4 %fusion.185 = f32[3,2048]{1,0:T(4,128)S(1)} fusion(f32[4,3,512]{2,1,0:T(4,128)S(1)} %dynamic-slice_bitcast_fusion.10, f32[512]{0:T(512)S(1)} %bitcast.259, f32[512]{0:T(512)S(1)} %bitcast.258, f32[4,512]{1,0:T(4,128)S(1)} %dynamic-slice_bitcast_fusion.11, f32[2048]{0:T(1024)S(1)} %bitcast.251, f32[4,512]{1,0:T(4,128)S(1)} %get-tuple-element.324, ...), kind=kOutput, calls=%fused_computation.39.clone.2 | convolution fusion | flops 197144576 | bytes 143361 | tf_op jit(solution)/shard_map/while/body/eval_jaxpr/scr,sra->ca/dot_general | solution.py:178
  417.4 74.4 %fusion.185 = f32[3,2048]{1,0:T(4,128)S(1)} fusion(f32[4,3,512]{2,1,0:T(4,128)S(1)} %dynamic-slice_bitcast_fusion.10, f32[512]{0:T(512)S(1)} %bitcast.259, f32[512]{0:T(512)S(1)} %bitcast.258, f32[4,512]{1,0:T(4,128)S(1)} %dynamic-slice_bitcast_fusion.11, f32[2048]{0:T(1024)S(1)} %bitcast.251, f32[4,512]{1,0:T(4,128)S(1)} %get-tuple-element.324, ...), kind=kOutput, calls=%fused_computation.39.clone.2 | convolution fusion | flops 197144576 | bytes 143361 | tf_op jit(solution)/shard_map/while/body/eval_jaxpr/scr,sra->ca/dot_general | solution.py:178
  491.8 13.9 %psum.15 = f32[3,2048]{1,0:T(4,128)} all-reduce(f32[3,2048]{1,0:T(4,128)S(1)} %get-tuple-element.73), channel_id=1, replica_groups=mesh['refl'=4,'atom'=32] {'refl'}, use_global_device_ids=true, to_apply=%region_15.16 | all-reduce | flops 6144 | bytes 49152 | tf_op jit(solution)/shard_map/psum | solution.py:187
  (153 shorter events, 33.7 us)
Async XLA Ops:
  0.6 96.4 %copy-start = (f32[4,3]{1,0:T(4,128)S(1)}, f32[4,3]{1,0:T(4,128)}, u32[]{:S(2)}) copy-start(f32[4,3]{1,0:T(4,128)} %param.27) | copy-start | bytes 148
  0.6 8.6 %copy-start.15 = (s32[1,32]{1,0:T(1,128)S(1)}, s32[1,32]{1,0:T(1,128)}, u32[]{:S(2)}) copy-start(s32[1,32]{1,0:T(1,128)} %param.24) | copy-start | bytes 388
  0.7 8.6 %copy-start.11 = (s32[4,3,3]{2,0,1:T(4,128)S(1)}, s32[4,3,3]{2,0,1:T(4,128)}, u32[]{:S(2)}) copy-start(s32[4,3,3]{2,0,1:T(4,128)} %param.26) | copy-start | bytes 436
  0.7 8.7 %copy-start.7 = (s32[3,1024]{1,0:T(4,128)S(1)}, s32[3,1024]{1,0:T(4,128)}, u32[]{:S(2)}) copy-start(s32[3,1024]{1,0:T(4,128)} %param.25) | copy-start | bytes 36868
  4.3 5.7 %collective-permute-start = (bf16[48,64]{0,1:T(8,128)(2,1)S(1)}, bf16[48,64]{0,1:T(8,128)(2,1)S(1)}, u32[]{:S(2)}, u32[]{:S(2)}) collective-permute-start(bf16[48,64]{0,1:T(8,128)(2,1)S(1)} %get-tuple-element.188), channel_id=1, source_target_pairs={{0,1},{1,2},{2,3},{3,4},{4,5},{5,6},{6,7},{7,8},{8,9},{9,10},{10,1... | collective-permute-start | bytes 18440 | tf_op jit(solution)/shard_map/ppermute | solution.py:22
  7.9 5.8 %collective-permute-start.1 = (bf16[48,64]{0,1:T(8,128)(2,1)S(1)}, bf16[48,64]{0,1:T(8,128)(2,1)S(1)}, u32[]{:S(2)}, u32[]{:S(2)}) collective-permute-start(bf16[48,64]{0,1:T(8,128)(2,1)S(1)} %get-tuple-element.189), channel_id=1, source_target_pairs={{1,0},{2,1},{3,2},{4,3},{5,4},{6,5},{7,6},{8,7},{9,8},{10,9},{11,1... | collective-permute-start | bytes 18440 | tf_op jit(solution)/shard_map/ppermute | solution.py:24
  18.2 7.2 %copy-start.2 = (bf16[64,32,32]{1,2,0:T(8,128)(2,1)S(1)}, bf16[64,32,32]{1,2,0:T(8,128)(2,1)}, u32[]{:S(2)}) copy-start(bf16[64,32,32]{1,2,0:T(8,128)(2,1)} %copy.108) | copy-start | bytes 393220
  24.3 4.3 copy-start.3
  28.6 11.9 %copy-start.5 = (bf16[2,128,128]{2,1,0:T(8,128)(2,1)S(1)}, bf16[2,128,128]{2,1,0:T(8,128)(2,1)}, u32[]{:S(2)}) copy-start(bf16[2,128,128]{2,1,0:T(8,128)(2,1)} %param.20) | copy-start | bytes 196612
  31.6 15.7 %copy-start.10 = (f32[2048]{0:T(1024)S(1)}, f32[2048]{0:T(1024)}, u32[]{:S(2)}) copy-start(f32[2048]{0:T(1024)} %param.23) | copy-start | bytes 24580
  41.6 6.6 %collective-permute-start.2 = (bf16[48,64]{0,1:T(8,128)(2,1)S(1)}, bf16[48,64]{0,1:T(8,128)(2,1)S(1)}, u32[]{:S(2)}, u32[]{:S(2)}) collective-permute-start(bf16[48,64]{0,1:T(8,128)(2,1)S(1)} %get-tuple-element.184), channel_id=1, source_target_pairs={{0,1},{1,2},{2,3},{3,4},{4,5},{5,6},{6,7},{7,8},{8,9},{9,10},{10,1... | collective-permute-start | bytes 18440 | tf_op jit(solution)/shard_map/ppermute | solution.py:22
  45.5 5.6 %collective-permute-start.3 = (bf16[48,64]{0,1:T(8,128)(2,1)S(1)}, bf16[48,64]{0,1:T(8,128)(2,1)S(1)}, u32[]{:S(2)}, u32[]{:S(2)}) collective-permute-start(bf16[48,64]{0,1:T(8,128)(2,1)S(1)} %get-tuple-element.185), channel_id=1, source_target_pairs={{1,0},{2,1},{3,2},{4,3},{5,4},{6,5},{7,6},{8,7},{9,8},{10,9},{11,1... | collective-permute-start | bytes 18440 | tf_op jit(solution)/shard_map/ppermute | solution.py:24
  53.5 5.8 %copy-start.4 = (bf16[2048,32]{0,1:T(8,128)(2,1)S(1)}, bf16[2048,32]{0,1:T(8,128)(2,1)}, u32[]{:S(2)}) copy-start(bf16[2048,32]{0,1:T(8,128)(2,1)} %get-tuple-element.166) | copy-start | bytes 393220
  70.4 12.6 %copy-start.9 = (f32[3,2048]{1,0:T(4,128)S(1)}, f32[3,2048]{1,0:T(4,128)}, u32[]{:S(2)}) copy-start(f32[3,2048]{1,0:T(4,128)} %param.22) | copy-start | bytes 73732
  70.4 12.6 %copy-start.14 = (bf16[3,128]{1,0:T(4,128)(2,1)S(1)}, bf16[3,128]{1,0:T(4,128)(2,1)}, u32[]{:S(2)}) copy-start(bf16[3,128]{1,0:T(4,128)(2,1)} %param.21) | copy-start | bytes 2308
  70.4 12.9 %copy-start.6 = (f32[1,32,64]{2,0,1:T(1,128)S(1)}, f32[1,32,64]{2,0,1:T(1,128)}, u32[]{:S(2)}) copy-start(f32[1,32,64]{2,0,1:T(1,128)} %concatenate.76) | copy-start | bytes 24580
  73.3 23.7 %copy-start.8 = (s32[3,1024]{1,0:T(4,128)S(1)}, s32[3,1024]{1,0:T(4,128)}, u32[]{:S(2)}) copy-start(s32[3,1024]{1,0:T(4,128)} %param.25) | copy-start | bytes 36868
  84.8 20.5 %all-to-all-start = ((f32[32,1,256]{2,1,0:T(1,128)}), f32[32,1,256]{2,1,0:T(1,128)S(1)}, u32[]{:S(2)}, u32[]{:S(2)}) async-start(f32[32,1,256]{2,1,0:T(1,128)} %reshape.358), calls=%async_computation | async-start | bytes 65536 | tf_op jit(solution)/shard_map/all_to_all | solution.py:131
  106.8 235.7 %copy-start.12 = (f32[1024]{0:T(1024)S(1)}, f32[1024]{0:T(1024)}, u32[]{:S(2)}) copy-start(f32[1024]{0:T(1024)} %param.28) | copy-start | bytes 12292
  106.8 235.7 %copy-start.13 = (f32[1024]{0:T(1024)S(1)}, f32[1024]{0:T(1024)}, u32[]{:S(2)}) copy-start(f32[1024]{0:T(1024)} %param.29) | copy-start | bytes 12292
  177.4 3.6 copy-start.1
  255.2 3.6 copy-start.1
where the time goes:
time: 516 us; the launch traced here: 507 us
  matrix products  177 us (34%)
  other arithmetic  143 us (28%)
  blocking collectives  111 us (22%)
  local copies, waits for them, and re-layouts  37.5 us (7%)
  starting transfers between devices  22.7 us (4%)
  waiting for transfers between devices  13.5 us (3%)
    dot_general x2, matrix products, accumulate(): jnp.einsum('scr,sra->ca', hs_blk, coef, precision=lax.Precision.HIGHEST)  149 us
    reduce_sum x2, other arithmetic, structure(): fa = jnp.einsum('sra,a->r', cosv, power, precision=lax.Precision.HIGHEST)  141 us
    psum x1, blocking collectives, body(): totals = lax.psum(partial_sums, 'atom')  80 us
    reshape x32, local copies, waits for them, and re-layouts, window_blocks(): padded[QWIN * j:QWIN * j + window_count * QWIN]  25.5 us
    all_gather x2, blocking collectives, body(): lax.all_gather(head_rows, 'refl', axis=1, tiled=True)  17 us
    psum x1, blocking collectives, body(): coord_grad = lax.psum(local_grad, 'refl')  13.9 us
    all_to_all x1, starting transfers between devices, body(): lax.all_to_all(packed, 'atom', split_axis=1, concat_axis=1, tiled=True)  12.2 us
  transfers between devices with their start and end apart: 5, of which 3 were waited for; matrix products, arithmetic and copies ran while one was open for 1% of the time, Pallas kernels for 0%

commit v1 on v0

v1 whole, which is shorter than its diff:
```python
import functools
import math

import jax
import jax.numpy as jnp
from jax import lax
from jax.experimental import pallas as pl
from jax.experimental.pallas import tpu as pltpu
from jax.sharding import PartitionSpec as P

HEAD = 32
QWIN = 32
KWIN = 128
BORDER = (KWIN - QWIN) // 2
LAYERS = 2
HALO = 128
TOP = 12
ROWS = 640
BF = jnp.bfloat16
F32 = jnp.float32
LANES = (((1,), (1,)), ((), ()))


def dot(a, b, dims=(((1,), (0,)), ((), ()))):
    return lax.dot_general(a, b, dims, preferred_element_type=F32)


def cos_turns(t):
    t = t - jnp.round(t)
    s = 0.25 - jnp.abs(t)
    z = s * s
    p = 81.6010046 + z * (39.5368083 * z - 76.5497956)
    return s * (6.28318516 + z * (z * p - 41.341655))


def full_terms(x):
    i = lax.broadcasted_iota(jnp.int32, (32, 1), 0)
    sine = i > TOP
    freq = jnp.where(sine, i - TOP, i).astype(F32)
    shift = jnp.where(sine, 0.25, 0.0).astype(F32)
    live = jnp.where(i <= 2 * TOP, 1.0, 0.0).astype(F32)
    return cos_turns(freq * x - shift) * live


def part_terms(x):
    i = lax.broadcasted_iota(jnp.int32, (2 * TOP, 1), 0)
    sine = i >= TOP
    freq = jnp.where(sine, i - TOP + 1, i + 1).astype(F32)
    shift = jnp.where(sine, 0.25, 0.0).astype(F32)
    return cos_turns(freq * x - shift)


def fill_products(p_ref, v, w):
    for j in range(TOP):
        a = v[2 * j : 2 * j + 1] * w
        b = v[2 * j + 1 : 2 * j + 2] * w
        p_ref[48 * j : 48 * j + 48, :] = jnp.concatenate([a, b], axis=0).astype(BF)
    last = v[24:25] * w
    pad = jnp.zeros((8, v.shape[1]), F32)
    p_ref[576:640, :] = jnp.concatenate([last, v, pad], axis=0).astype(BF)


def picks(m, rows, first):
    i = lax.broadcasted_iota(jnp.int32, (rows, m.shape[1]), 0) + first
    size = jnp.abs(m)
    sign = jnp.clip(m, -1, 1).astype(F32)
    return (
        jnp.where(i == size, 1.0, 0.0).astype(F32),
        jnp.where(i == size + TOP, sign, 0.0).astype(F32),
    )


def fill_picks(re_ref, im_ref, k, l):
    ck, sk = picks(k, 32, 0)
    cl, sl = picks(l, 2 * TOP, 1)
    flat = jnp.where(l == 0, 1.0, 0.0).astype(F32)

    def real(j):
        return ck[j : j + 1] * cl - sk[j : j + 1] * sl

    def imag(j):
        return ck[j : j + 1] * sl + sk[j : j + 1] * cl

    pad = jnp.zeros((8, k.shape[1]), F32)
    for ref, own, tail in ((re_ref, real, ck * flat), (im_ref, imag, sk * flat)):
        for j in range(TOP):
            pair = jnp.concatenate([own(2 * j), own(2 * j + 1)], axis=0)
            ref[48 * j : 48 * j + 48, :] = pair.astype(BF)
        ref[576:640, :] = jnp.concatenate([own(24), tail, pad], axis=0).astype(BF)


def split(a, count):
    parts = []
    for _ in range(count):
        hi = a.astype(BF)
        parts.append(hi)
        a = a - hi.astype(F32)
    return jnp.concatenate(parts, axis=0)


def images(pos, rot_ref, shf_ref, s):
    rows = []
    for k in range(3):
        r = shf_ref[s, k] + rot_ref[s, 3 * k].astype(F32) * pos[0:1]
        r = r + rot_ref[s, 3 * k + 1].astype(F32) * pos[1:2]
        rows.append(r + rot_ref[s, 3 * k + 2].astype(F32) * pos[2:3])
    return rows


def attend_kernel(
    natom,
    norm,
    nops,
    span,
    rank_ref,
    route_ref,
    rot_ref,
    shf_ref,
    prev_ref,
    feat_ref,
    next_ref,
    wqkv_ref,
    wout_ref,
    gain_ref,
    wcoord_ref,
    noisy_ref,
    power_ref,
    miller_ref,
    out_ref,
    pay_ref,
    x_ref,
    q_ref,
    k_ref,
    v_ref,
    pos_ref,
    p_ref,
    g_ref,
    re_ref,
    im_ref,
    f_ref,
):
    local = feat_ref.shape[0]
    x_ref[0:HALO, :] = prev_ref[...].astype(F32)
    x_ref[HALO : HALO + local, :] = feat_ref[...].astype(F32)
    x_ref[HALO + local :, :] = next_ref[...].astype(F32)
    origin = rank_ref[0] * local - HALO
    head_of = lax.broadcasted_iota(jnp.int32, (QWIN, 128), 1) // HEAD
    lane = lax.broadcasted_iota(jnp.int32, (1, KWIN), 1)
    scale = HEAD**-0.5 * math.log2(math.e)

    for layer in range(LAYERS):
        edge = 64 * layer
        weights = jnp.concatenate(
            [wqkv_ref[g, layer, j] for j in range(3) for g in range(4)], axis=0
        )
        gain = gain_ref[layer : layer + 1, :]

        def project(i, _):
            r = pl.multiple_of(edge + i * 128, 64)
            xc = x_ref[pl.ds(r, 128), :]
            cent = xc - jnp.mean(xc, axis=1, keepdims=True)
            var = jnp.mean(cent * cent, axis=1, keepdims=True)
            normed = (cent * lax.rsqrt(var + 1e-05) * gain).astype(BF)
            proj = dot(normed, weights, LANES).astype(BF)
            q_ref[pl.ds(r, 128), :] = proj[:, 0:128]
            k_ref[pl.ds(r, 128), :] = proj[:, 128:256]
            v_ref[pl.ds(r, 128), :] = proj[:, 256:384]
            return 0

        lax.fori_loop(0, (local + 2 * HALO) // 128 - layer, project, 0)
        w_out = wout_ref[layer]
        first = 64 * (layer + 1)

        def attend(i, _):
            base = pl.multiple_of(first + i * 128, 64)
            heads = []
            for win in range(4):
                r = base + win * QWIN
                qw = q_ref[pl.ds(pl.multiple_of(r, 32), QWIN), :]
                at = pl.multiple_of(r - BORDER, 16)
                kw = k_ref[pl.ds(at, KWIN), :]
                vw = v_ref[pl.ds(at, KWIN), :]
                qm = jnp.concatenate(
                    [jnp.where(head_of == h, qw, jnp.zeros_like(qw)) for h in range(4)], axis=0
                )
                s = dot(qm, kw, LANES)
                place = lane + (origin + at)
                s = jnp.where((place >= 0) & (place < natom), s, -1e30)
                e = jnp.exp2((s - jnp.max(s, axis=1, keepdims=True)) * scale)
                probs = (e / jnp.sum(e, axis=1, keepdims=True)).astype(BF)
                o = dot(probs, vw)
                own = jnp.zeros((QWIN, 128), F32)
                for h in range(4):
                    own = jnp.where(head_of == h, o[QWIN * h : QWIN * h + QWIN], own)
                heads.append(own.astype(BF))
            y = dot(jnp.concatenate(heads, axis=0), w_out)
            x_ref[pl.ds(base, 128), :] += y
            return 0

        lax.fori_loop(0, local // 128 + 1 - layer, attend, 0)

    pos_ref[...] = jnp.zeros_like(pos_ref)
    pos_ref[3:4, :] = power_ref[...]
    step = 256
    for i in range(local // step):
        at = slice(i * step, (i + 1) * step)
        done = x_ref[HALO + i * step : HALO + (i + 1) * step, :].astype(BF)
        out_ref[at, :] = done
        pos_ref[0:3, at] = noisy_ref[:, at] + 0.02 * dot(wcoord_ref[...], done, LANES)

    g_ref[...] = jnp.zeros_like(g_ref)
    chunks = local // span

    def sums(i, _):
        s = i // chunks
        at = pl.multiple_of((i % chunks) * span, span)
        pos = pos_ref[:, pl.ds(at, span)]
        x0, x1, x2 = images(pos, rot_ref, shf_ref, s)
        u = split(full_terms(x0) * pos[3:4], 2)
        fill_products(p_ref, full_terms(x1), part_terms(x2))
        g_ref[...] += dot(u, p_ref[...], LANES)
        return 0

    lax.fori_loop(0, nops * chunks, sums, 0)
    grid = split(g_ref[0:32, :] + g_ref[32:64, :], 3)
    group = miller_ref.shape[1]
    wide = re_ref.shape[1]
    for c in range(group // wide):
        m = miller_ref[:, c * wide : (c + 1) * wide]
        fill_picks(re_ref, im_ref, m[1:2], m[2:3])
        yr = dot(grid, re_ref[...])
        yi = dot(grid, im_ref[...])
        yr = yr[0:32] + yr[32:64] + yr[64:96]
        yi = yi[0:32] + yi[32:64] + yi[64:96]
        uc, us = picks(m[0:1], 32, 0)
        fa = jnp.sum(uc * yr - us * yi, axis=0, keepdims=True) * norm
        fb = jnp.sum(uc * yi + us * yr, axis=0, keepdims=True) * norm
        for b in range(wide // 128):
            row = c * (wide // 128) + b
            f_ref[row : row + 1, :] = fa[:, b * 128 : (b + 1) * 128]
            f_ref[row + 8 : row + 9, :] = fb[:, b * 128 : (b + 1) * 128]

    both = f_ref[...]
    for e in range(pay_ref.shape[0]):
        blk = route_ref[0, e]
        at = pl.multiple_of((blk // 2) * 128, 128)
        piece = pos_ref[:, pl.ds(at, 128)]
        odd = jnp.full(piece.shape, blk % 2, jnp.int32) == 1
        pay_ref[e, 0:16, :] = both
        pay_ref[e, 16:24, :] = jnp.where(odd, pltpu.roll(piece, 64, 1), piece)


def gradient_kernel(
    nrefl,
    norm,
    nops,
    span,
    rot_ref,
    shf_ref,
    recv_ref,
    miller_ref,
    obs_ref,
    wt_ref,
    amp_ref,
    grad_ref,
    pos_ref,
    p_ref,
    w_ref,
    re_ref,
    im_ref,
):
    shards = recv_ref.shape[0]
    total = recv_ref[0, 0:16, :]
    for e in range(1, shards):
        total = total + recv_ref[e, 0:16, :]
    fa, fb = total[0:8], total[8:16]
    amp = jnp.sqrt(fa * fa + fb * fb + 1.0)
    slope = 2.0 * wt_ref[...] * (amp - obs_ref[...]) / (amp * math.sqrt(nrefl))
    amp_ref[...] = amp
    ga, gb = slope * fa, slope * fb
    left = lax.broadcasted_iota(jnp.int32, (8, 128), 1) < 64
    for j in range(shards // 2):
        other = pltpu.roll(recv_ref[2 * j + 1, 16:24, :], 64, 1)
        pos_ref[:, 128 * j : 128 * j + 128] = jnp.where(left, recv_ref[2 * j, 16:24, :], other)

    group = miller_ref.shape[1]
    wide = re_ref.shape[1]
    rows = wide // 128
    for c in range(group // wide):
        m = miller_ref[:, c * wide : (c + 1) * wide]
        fill_picks(re_ref, im_ref, m[1:2], m[2:3])
        uc, us = picks(m[0:1], 32, 0)
        a = jnp.concatenate([ga[c * rows + b : c * rows + b + 1] for b in range(rows)], axis=1)
        b = jnp.concatenate([gb[c * rows + b : c * rows + b + 1] for b in range(rows)], axis=1)
        real = b * uc - a * us
        imag = -(a * uc + b * us)
        mf = m.astype(F32)
        real = split(jnp.concatenate([mf[k : k + 1] * real for k in range(3)], axis=0), 2)
        imag = split(jnp.concatenate([mf[k : k + 1] * imag for k in range(3)], axis=0), 2)
        part = dot(real, re_ref[...], LANES) + dot(imag, im_ref[...], LANES)
        part = part[0:96] + part[96:192]
        w_ref[...] = part if c == 0 else w_ref[...] + part
    coef = split(w_ref[...], 2)
    local = pos_ref.shape[1]
    grad_ref[...] = jnp.zeros_like(grad_ref)
    chunks = local // span
    factor = 2.0 * math.pi * norm

    def slopes(i, _):
        s = i // chunks
        at = pl.multiple_of((i % chunks) * span, span)
        pos = pos_ref[:, pl.ds(at, span)]
        x0, x1, x2 = images(pos, rot_ref, shf_ref, s)
        u = full_terms(x0)
        fill_products(p_ref, full_terms(x1), part_terms(x2))
        t = dot(coef, p_ref[...])
        t = t[0:96] + t[96:192]
        scale = pos[3:4] * factor
        g = [jnp.sum(u * t[32 * k : 32 * k + 32], axis=0, keepdims=True) * scale for k in range(3)]
        for c in range(3):
            r = rot_ref[s, c].astype(F32) * g[0]
            r = r + rot_ref[s, 3 + c].astype(F32) * g[1]
            r = r + rot_ref[s, 6 + c].astype(F32) * g[2]
            grad_ref[c : c + 1, pl.ds(at, span)] += r
        return 0

    lax.fori_loop(0, nops * chunks, slopes, 0)


def body(
    features,
    ln_gain,
    w_qkv,
    w_out,
    w_coord,
    noisy_coords,
    scatter_power,
    route,
    miller,
    rotations,
    shifts,
    observed,
    obs_weight,
):
    shards = lax.axis_size("atom")
    rank = lax.axis_index("atom")
    local = features.shape[0]
    natom = local * shards
    group = miller.shape[1]
    nops = rotations.shape[0]
    nrefl = group * lax.axis_size("refl")
    norm = 1.0 / math.sqrt(nops * natom)
    span = 512
    wide = 256
    smem = pl.BlockSpec(memory_space=pltpu.SMEM)
    vmem = pl.BlockSpec(memory_space=pltpu.VMEM)

    ends = shards - 1
    before = lax.ppermute(features[local - HALO :], "atom", [(i, i + 1) for i in range(ends)])
    after = lax.ppermute(features[:HALO], "atom", [(i + 1, i) for i in range(ends)])
    weights = lax.all_gather(w_qkv.transpose(0, 1, 3, 2), "refl")
    rot = rotations.reshape(nops, 9)
    params = pltpu.CompilerParams(vmem_limit_bytes=60 * 1024 * 1024)
    atom_out, payload = pl.pallas_call(
        functools.partial(attend_kernel, natom, norm, nops, span),
        out_shape=(
            jax.ShapeDtypeStruct((local, 128), BF),
            jax.ShapeDtypeStruct((shards, 24, 128), F32),
        ),
        in_specs=[smem] * 4 + [vmem] * 10,
        out_specs=(vmem, vmem),
        scratch_shapes=[
            pltpu.VMEM((local + 2 * HALO, 128), F32),
            pltpu.VMEM((local + 2 * HALO, 128), BF),
            pltpu.VMEM((local + 2 * HALO, 128), BF),
            pltpu.VMEM((local + 2 * HALO, 128), BF),
            pltpu.VMEM((8, local), F32),
            pltpu.VMEM((ROWS, span), BF),
            pltpu.VMEM((64, ROWS), F32),
            pltpu.VMEM((ROWS, wide), BF),
            pltpu.VMEM((ROWS, wide), BF),
            pltpu.VMEM((16, 128), F32),
        ],
        compiler_params=params,
        name="attend",
    )(
        rank.reshape(1),
        route,
        rot,
        shifts,
        before,
        features,
        after,
        weights,
        w_out,
        ln_gain,
        w_coord,
        noisy_coords,
        scatter_power[None, :],
        miller,
    )
    recv = lax.all_to_all(payload, "atom", split_axis=0, concat_axis=0, tiled=True)
    amp, grad = pl.pallas_call(
        functools.partial(gradient_kernel, nrefl, norm, nops, span),
        out_shape=(
            jax.ShapeDtypeStruct((8, 128), F32),
            jax.ShapeDtypeStruct((3, local), F32),
        ),
        in_specs=[smem] * 2 + [vmem] * 4,
        out_specs=(vmem, vmem),
        scratch_shapes=[
            pltpu.VMEM((8, local), F32),
            pltpu.VMEM((ROWS, span), BF),
            pltpu.VMEM((96, ROWS), F32),
            pltpu.VMEM((ROWS, wide), BF),
            pltpu.VMEM((ROWS, wide), BF),
        ],
        compiler_params=params,
        name="gradient",
    )(rot, shifts, recv, miller, observed.reshape(8, 128), obs_weight.reshape(8, 128))
    grad = grad + lax.ppermute(grad, "refl", [(0, 1), (1, 0), (2, 3), (3, 2)])
    grad = grad + lax.ppermute(grad, "refl", [(0, 2), (2, 0), (1, 3), (3, 1)])
    share = group // shards
    amplitude = lax.dynamic_slice_in_dim(amp.reshape(group), rank * share, share, 0)
    return (atom_out, amplitude, grad)


def solution(mesh):
    placed = (
        P("atom", None),
        P(),
        P(None, None, None, "refl"),
        P(),
        P(),
        P(None, "atom"),
        P("atom"),
        P("atom", None),
        P(None, "refl"),
        P(),
        P(),
        P("refl"),
        P("refl"),
    )
    return jax.shard_map(
        body,
        mesh=mesh,
        in_specs=placed,
        out_specs=(P("atom", None), P(("refl", "atom")), P(None, "atom")),
        check_vma=False,
    )
```

time: 516 us -> 129 us (0.25); the launches traced: 507 us -> 128 us
  matrix products: 177 us -> 0 us
  other arithmetic: 143 us -> 1.39 us
  Pallas kernels: 0 us -> 80.5 us
  blocking collectives: 111 us -> 30.8 us
  local copies, waits for them, and re-layouts: 37.5 us -> 3.33 us
  starting transfers between devices: 22.7 us -> 8.81 us
  waiting for transfers between devices: 13.5 us -> 2.68 us
    dot_general x13 -> x0, matrix products: 170 us -> none  [the longest x2 149 us: accumulate(): jnp.einsum('scr,sra->ca', hs_blk, coef, precision=lax.Precision.HIGHEST)]
    reduce_sum x5 -> x0, other arithmetic: 141 us -> none  [the longest x2 141 us: structure(): fa = jnp.einsum('sra,a->r', cosv, power, precision=lax.Precision.HIGHEST)]
    psum x2 -> x0, blocking collectives: 93.9 us -> none  [the longest x1 80 us: body(): totals = lax.psum(partial_sums, 'atom')]
    pallas_call x0 -> x2, Pallas kernels: none -> 80.5 us  [the longest x1 71.1 us: body(): pl.pallas_call(functools.partial(attend_kernel, natom, norm, nops, span),...]
    reshape x35 -> x1, local copies, waits for them, and re-layouts: 25.6 us -> 0.65 us  [body(): rot = rotations.reshape(nops, 9)]
    all_to_all x0 -> x1, blocking collectives: none -> 23.2 us  [body(): lax.all_to_all(payload, 'atom', split_axis=0, concat_axis=0, tiled=True)]
    all_to_all x1 -> x0, starting transfers between devices: 12.2 us -> none  [body(): lax.all_to_all(packed, 'atom', split_axis=1, concat_axis=1, tiled=True)]
    all_gather x2 -> x1, blocking collectives: 17 us -> 7.65 us  [body(): weights = lax.all_gather(w_qkv.transpose(0, 1, 3, 2), 'refl')]
  transfers between devices with their start and end apart: 5 -> 4, of which waited for: 3 -> 2; matrix products, arithmetic and copies ran while one was open for 1% -> 1% of each run, Pallas kernels for 0% -> 0%
where the time goes in v1:
time: 129 us; the launch traced here: 128 us
  Pallas kernels  80.5 us (62%)
  blocking collectives  30.8 us (24%)
  starting transfers between devices  8.81 us (7%)
  local copies, waits for them, and re-layouts  3.33 us (3%)
  waiting for transfers between devices  2.68 us (2%)
  other arithmetic  1.39 us (1%)
    pallas_call x1, Pallas kernels, body(): pl.pallas_call(functools.partial(attend_kernel, natom, norm, nops, span),...  71.1 us
    all_to_all x1, blocking collectives, body(): lax.all_to_all(payload, 'atom', split_axis=0, concat_axis=0, tiled=True)  23.2 us
    pallas_call x1, Pallas kernels, body(): pl.pallas_call(functools.partial(gradient_kernel, nrefl, norm, nops, span...  9.37 us
    all_gather x1, blocking collectives, body(): weights = lax.all_gather(w_qkv.transpose(0, 1, 3, 2), 'refl')  7.65 us
    ppermute x1, starting transfers between devices, body(): lax.ppermute(features[local - HALO:], 'atom', [(i, i + 1) for i in range(...  4.55 us
    ppermute x1, starting transfers between devices, body(): grad = grad + lax.ppermute(grad, 'refl', [(0, 2), (2, 0), (1, 3), (3, 1)])  2.98 us
  transfers between devices with their start and end apart: 4, of which 2 were waited for; matrix products, arithmetic and copies ran while one was open for 1% of the time, Pallas kernels for 0%

profile of v1, /device:TPU:0, one launch (start us, length us, event | category | flops | bytes accessed | tf_op | source)
XLA Modules:
  0.0 128.2 jit_solution(2655100747613130086)
XLA Ops:
  0.6 0.0 copy-start
  0.6 0.8 fusion
  1.4 1.3 collective-permute-start.1
  2.7 4.5 %collective-permute-start = (bf16[128,128]{1,0:T(8,128)(2,1)S(1)}, bf16[128,128]{1,0:T(8,128)(2,1)S(1)}, u32[]{:S(2)}, u32[]{:S(2)}) collective-permute-start(bf16[128,128]{1,0:T(8,128)(2,1)S(1)} %get-tuple-element.12), channel_id=1, source_target_pairs={{0,1},{1,2},{2,3},{3,4},{4,5},{5,6},{6,7},{7,8},{8,9},{9,10},{10,1... | collective-permute-start | bytes 98312 | tf_op jit(solution)/shard_map/ppermute | solution.py:359
  7.3 0.0 copy-done
  7.3 0.0 copy-start.3
  7.3 7.7 %all-gather = bf16[8,3,32,128]{3,2,1,0:T(8,128)(2,1)} all-gather(bf16[2,3,32,128]{3,2,1,0:T(8,128)(2,1)S(1)} %bitcast.8), channel_id=2, replica_groups=mesh['refl'=4,'atom'=32] {'refl'}, dimensions={0}, use_global_device_ids=true | all-gather | bytes 245760 | tf_op jit(solution)/shard_map/all_gather | solution.py:361
  15.0 0.0 copy-done.3
  15.0 0.6 reshape.22.rot_ref
  15.6 0.0 collective-permute-done.1.next_ref
  15.6 0.0 copy-start.1
  15.6 0.0 collective-permute-done.prev_ref
  15.6 0.0 copy-start.2
  15.6 0.6 copy-done.1
  16.2 0.0 copy-done.2
  16.2 71.1 %attend.1 = (bf16[2048,128]{1,0:T(8,128)(2,1)}, f32[32,24,128]{2,1,0:T(8,128)}) custom-call(s32[1]{0:T(128)} %bitcast.rank_ref, s32[1,32]{1,0:T(1,128)} %route_ref.1, s32[4,9]{1,0:T(4,128)} %reshape.22.rot_ref, f32[4,3]{1,0:T(4,128)} %shf_ref.3, bf16[128,128]{1,0:T(8,128)(2,1)} %copy-done.2, bf16[2048,128]{1,0:T(8,128)(2,1)} %feat_ref.1, ...), custom_call_target="tpu_custom_call" | custom-call | tf_op jit(solution)/shard_map/attend/pallas_call | solution.py:364
  87.4 23.2 %all_to_all.5.recv_ref = f32[32,24,128]{2,1,0:T(8,128)} all-to-all(f32[32,24,128]{2,1,0:T(8,128)} %get-tuple-element.8), channel_id=1, replica_groups=mesh['refl'=4,'atom'=32] {'atom'}, dimensions={0} | all-to-all | bytes 786432 | tf_op jit(solution)/shard_map/all_to_all | solution.py:402
  110.6 9.4 %gradient.1 = (f32[8,128]{1,0:T(8,128)}, f32[3,2048]{1,0:T(4,128)}) custom-call(s32[4,9]{1,0:T(4,128)} %reshape.22.rot_ref, f32[4,3]{1,0:T(4,128)} %shf_ref.3, f32[32,24,128]{2,1,0:T(8,128)} %all_to_all.5.recv_ref, s32[3,1024]{1,0:T(4,128)} %miller_ref.3, f32[8,128]{1,0:T(8,128)} %bitcast.10, f32[8,128]{1,0:T(8,128)} %bitcast.11), custom_call_target="tpu_custom_call" | custom-call | tf_op jit(solution)/shard_map/gradient/pallas_call | solution.py:403
  119.9 0.0 collective-permute-start.2
  119.9 1.4 %collective-permute-done.2 = f32[3,2048]{1,0:T(4,128)S(1)} collective-permute-done((f32[3,2048]{1,0:T(4,128)}, f32[3,2048]{1,0:T(4,128)S(1)}, u32[]{:S(2)}, u32[]{:S(2)}) %collective-permute-start.2) | collective-permute-done | bytes 24608 | tf_op jit(solution)/shard_map/ppermute | solution.py:421
  121.3 0.8 add.10
  122.1 3.0 %collective-permute-start.3 = (f32[3,2048]{1,0:T(4,128)S(1)}, f32[3,2048]{1,0:T(4,128)S(1)}, u32[]{:S(2)}, u32[]{:S(2)}) collective-permute-start(f32[3,2048]{1,0:T(4,128)S(1)} %add.10), channel_id=1, source_target_pairs={{0,64},{64,0},{32,96},{96,32},{1,65},{65,1},{33,97},{97,33},{2,66}... | collective-permute-start | bytes 73736 | tf_op jit(solution)/shard_map/ppermute | solution.py:422
  125.1 1.3 dynamic_slice.3
  126.4 1.3 collective-permute-done.3
  127.6 0.6 add.11
  (1 shorter events, 0.0 us)
Async XLA Ops:
  0.6 6.6 %copy-start = (bf16[2,3,128,32]{2,3,1,0:T(8,128)(2,1)S(1)}, bf16[2,3,128,32]{2,3,1,0:T(8,128)(2,1)}, u32[]{:S(2)}) copy-start(bf16[2,3,128,32]{2,3,1,0:T(8,128)(2,1)} %param.15) | copy-start | bytes 147460
  1.4 14.2 %collective-permute-start.1 = (bf16[128,128]{1,0:T(8,128)(2,1)S(1)}, bf16[128,128]{1,0:T(8,128)(2,1)S(1)}, u32[]{:S(2)}, u32[]{:S(2)}) collective-permute-start(bf16[128,128]{1,0:T(8,128)(2,1)S(1)} %get-tuple-element.11), channel_id=1, source_target_pairs={{1,0},{2,1},{3,2},{4,3},{5,4},{6,5},{7,6},{8,7},{9,8},{10,9},{11,1... | collective-permute-start | bytes 98312 | tf_op jit(solution)/shard_map/ppermute | solution.py:360
  2.7 12.9 %collective-permute-start = (bf16[128,128]{1,0:T(8,128)(2,1)S(1)}, bf16[128,128]{1,0:T(8,128)(2,1)S(1)}, u32[]{:S(2)}, u32[]{:S(2)}) collective-permute-start(bf16[128,128]{1,0:T(8,128)(2,1)S(1)} %get-tuple-element.12), channel_id=1, source_target_pairs={{0,1},{1,2},{2,3},{3,4},{4,5},{5,6},{6,7},{7,8},{8,9},{9,10},{10,1... | collective-permute-start | bytes 98312 | tf_op jit(solution)/shard_map/ppermute | solution.py:359
  7.3 7.7 %copy-start.3 = (s32[4,3,3]{2,0,1:T(4,128)S(1)}, s32[4,3,3]{2,0,1:T(4,128)}, u32[]{:S(2)}) copy-start(s32[4,3,3]{2,0,1:T(4,128)} %param.22) | copy-start | bytes 436
  15.6 0.6 copy-start.1
  15.6 0.6 copy-start.2
  119.9 1.4 %collective-permute-start.2 = (f32[3,2048]{1,0:T(4,128)}, f32[3,2048]{1,0:T(4,128)S(1)}, u32[]{:S(2)}, u32[]{:S(2)}) collective-permute-start(f32[3,2048]{1,0:T(4,128)} %get-tuple-element.10), channel_id=1, source_target_pairs={{0,32},{32,0},{64,96},{96,64},{1,33},{33,1},{65,97},{97,65},{2,34}... | collective-permute-start | bytes 73736 | tf_op jit(solution)/shard_map/ppermute | solution.py:421
  122.1 5.5 %collective-permute-start.3 = (f32[3,2048]{1,0:T(4,128)S(1)}, f32[3,2048]{1,0:T(4,128)S(1)}, u32[]{:S(2)}, u32[]{:S(2)}) collective-permute-start(f32[3,2048]{1,0:T(4,128)S(1)} %add.10), channel_id=1, source_target_pairs={{0,64},{64,0},{32,96},{96,32},{1,65},{65,1},{33,97},{97,33},{2,66}... | collective-permute-start | bytes 73736 | tf_op jit(solution)/shard_map/ppermute | solution.py:422

commit v2 on v1

v2 whole, which is shorter than its diff:
```python
import functools
import math

import jax
import jax.numpy as jnp
from jax import lax
from jax.experimental import pallas as pl
from jax.experimental.pallas import tpu as pltpu
from jax.sharding import PartitionSpec as P

HEAD = 32
QWIN = 32
KWIN = 128
BORDER = (KWIN - QWIN) // 2
LAYERS = 2
HALO = 128
SPAN = 1024
TABLE_SPAN = 512
TOP = 12
ROWS = 640
BF = jnp.bfloat16
F32 = jnp.float32
LANES = (((1,), (1,)), ((), ()))


def dot(a, b, dims=(((1,), (0,)), ((), ()))):
    return lax.dot_general(a, b, dims, preferred_element_type=F32)


def cos_turns(t):
    t = t - jnp.round(t)
    s = 0.25 - jnp.abs(t)
    z = s * s
    p = 81.6010046 + z * (39.5368083 * z - 76.5497956)
    return s * (6.28318516 + z * (z * p - 41.341655))


COSINES = TOP + 1
ORDER = list(range(COSINES)) + list(range(17, 17 + TOP))


def part_rows(i):
    sine = i >= TOP
    freq = jnp.where(i >= 16, i - 15, jnp.where(sine, i - 3, i))
    return freq.astype(F32), sine


def prepare(pos_ref, tab_ref, span):
    row = lax.broadcasted_iota(jnp.int32, (8, span), 0)
    bits = [(row & (1 << b)) != 0 for b in range(3)]
    low = row < 4

    def fill(i, _):
        at = pl.multiple_of(i * span, span)
        x = pos_ref[:, pl.ds(at, span)]
        cos_x, sin_x = cos_turns(x), cos_turns(x - 0.25)
        for k in range(3):
            c1 = jnp.broadcast_to(cos_x[k : k + 1], row.shape)
            s1 = jnp.broadcast_to(sin_x[k : k + 1], row.shape)
            c2, s2 = 1.0 - 2.0 * (s1 * s1), 2.0 * (s1 * c1)
            c4, s4 = 1.0 - 2.0 * (s2 * s2), 2.0 * (s2 * c2)
            c8, s8 = 1.0 - 2.0 * (s4 * s4), 2.0 * (s4 * c4)
            c, s = jnp.where(bits[0], c1, 1.0), jnp.where(bits[0], s1, 0.0)
            for bit, cm, sm in ((bits[1], c2, s2), (bits[2], c4, s4)):
                c, s = jnp.where(bit, c * cm - s * sm, c), jnp.where(bit, s * cm + c * sm, s)
            cb, sb = c * c8 - s * s8, s * c8 + c * s8
            cn, sn = c * c1 - s * s1, s * c1 + c * s1
            ct, st = cn * c8 - sn * s8, sn * c8 + cn * s8
            mid = jnp.where(low, cb, pltpu.roll(st, 4, 0))
            mid_other = jnp.where(low, sb, pltpu.roll(ct, 4, 0))
            for r, part in enumerate((c, cb, s, sb, c, mid, sn, s, mid_other, cn)):
                tab_ref[k, 8 * r : 8 * r + 8, pl.ds(at, span)] = part
        return 0

    lax.fori_loop(0, pos_ref.shape[1] // span, fill, 0)


def rotors(rot_ref, shf_ref, rotor_ref):
    lane = lax.broadcasted_iota(jnp.int32, (1, 128), 1)
    turn = jnp.zeros((1, 128), F32)
    sign = jnp.ones((1, 128), F32)
    nops = rotor_ref.shape[0]
    for s in range(nops):
        for k in range(3):
            here = lane == 3 * s + k
            whole = rot_ref[s, k, 0] + rot_ref[s, k, 1] + rot_ref[s, k, 2]
            turn = jnp.where(here, shf_ref[s, k], turn)
            sign = jnp.where(here, whole.astype(F32), sign)
    i = lax.broadcasted_iota(jnp.int32, (32, 1), 0)
    tables = [((i % 16).astype(F32), i >= 16)] * 2
    tables.append(part_rows(lax.broadcasted_iota(jnp.int32, (24, 1), 0)))
    for k, (freq, sine) in enumerate(tables):
        angle = freq * turn
        same = cos_turns(angle) * jnp.where(sine, sign, 1.0)
        other = cos_turns(angle - 0.25) * jnp.where(sine, 1.0, -sign)
        size = freq.shape[0]
        for s in range(nops):
            j = 3 * s + k
            spread = (size, 128)
            rotor_ref[s, 0, 32 * k : 32 * k + size, :] = jnp.broadcast_to(same[:, j : j + 1], spread)
            rotor_ref[s, 1, 32 * k : 32 * k + size, :] = jnp.broadcast_to(other[:, j : j + 1], spread)
    freq = jnp.full((8, 1), float(TOP), F32)
    same, other = cos_turns(freq * turn), cos_turns(freq * turn - 0.25) * -sign
    for s in range(nops):
        j = 3 * s + 2
        rotor_ref[s, 0, 88:96, :] = jnp.broadcast_to(same[:, j : j + 1], (8, 128))
        rotor_ref[s, 1, 88:96, :] = jnp.broadcast_to(other[:, j : j + 1], (8, 128))


def images(rot_ref, tab_ref, rotor_ref, v_ref, p_ref, s, at, span):
    def table(k, r, size):
        axis = jnp.abs(rot_ref[s, k, 1]) + 2 * jnp.abs(rot_ref[s, k, 2])
        return tab_ref[axis, r : r + size, pl.ds(at, span)]

    def factor(kind, r, size):
        return jnp.concatenate([rotor_ref[s, kind, r : r + size, :]] * (span // 128), axis=1)

    def both(k):
        c, n = table(k, 0, 16), table(k, 16, 16)
        cos = factor(0, 32 * k, 16) * c + factor(1, 32 * k, 16) * n
        sin = factor(0, 32 * k + 16, 16) * n + factor(1, 32 * k + 16, 16) * c
        return jnp.concatenate([cos, sin], axis=0)

    v = both(1)
    v_ref[...] = v
    w = factor(0, 64, 24) * table(2, 32, 24) + factor(1, 64, 24) * table(2, 56, 24)
    c12 = table(2, 8, 8)[4:5]
    s12 = table(2, 24, 8)[4:5]
    last = factor(0, 88, 8)[0:1] * c12 + factor(1, 88, 8)[0:1] * s12

    def row(j):
        return v_ref[ORDER[j] : ORDER[j] + 1, :]

    for j in range(TOP):
        pair = jnp.concatenate([row(2 * j) * w, row(2 * j + 1) * w], axis=0)
        p_ref[48 * j : 48 * j + 48, :] = pair.astype(BF)
    pad = jnp.zeros((8, span), F32)
    p_ref[576:640, :] = jnp.concatenate([row(24) * w, v * last, pad], axis=0).astype(BF)
    return both(0)


def picks(m):
    i = lax.broadcasted_iota(jnp.int32, (32, m.shape[1]), 0)
    size = jnp.abs(m)
    sign = jnp.clip(m, -1, 1).astype(F32)
    return (
        jnp.where(i == size, 1.0, 0.0).astype(F32),
        jnp.where(i == size + 16, sign, 0.0).astype(F32),
    )


def fill_picks(re_ref, im_ref, k, l):
    ck, sk = picks(k)
    i = lax.broadcasted_iota(jnp.int32, (24, l.shape[1]), 0)
    size = jnp.abs(l)
    sign = jnp.clip(l, -1, 1).astype(F32)
    cl = jnp.where(i == jnp.where(size < TOP, size, -1), 1.0, 0.0).astype(F32)
    sl = jnp.where(i == jnp.where(size >= 9, size + 3, size + 15), sign, 0.0).astype(F32)
    top = jnp.where(size == TOP, 1.0, 0.0).astype(F32)

    def real(j):
        r = ORDER[j]
        return ck[r : r + 1] * cl if r < 16 else -sk[r : r + 1] * sl

    def imag(j):
        r = ORDER[j]
        return ck[r : r + 1] * sl if r < 16 else sk[r : r + 1] * cl

    pad = jnp.zeros((8, k.shape[1]), F32)
    for ref, own, tail in ((re_ref, real, ck * top), (im_ref, imag, sk * top)):
        for j in range(TOP):
            pair = jnp.concatenate([own(2 * j), own(2 * j + 1)], axis=0)
            ref[48 * j : 48 * j + 48, :] = pair.astype(BF)
        ref[576:640, :] = jnp.concatenate([own(24), tail, pad], axis=0).astype(BF)


def split(a, count):
    parts = []
    for _ in range(count):
        hi = a.astype(BF)
        parts.append(hi)
        a = a - hi.astype(F32)
    return jnp.concatenate(parts, axis=0)


def attend_kernel(
    natom,
    nops,
    span,
    rot_ref,
    shf_ref,
    feat_ref,
    halo_ref,
    wqkv_ref,
    wout_ref,
    gain_ref,
    wcoord_ref,
    noisy_ref,
    power_ref,
    out_ref,
    half_ref,
    part_ref,
    x_ref,
    x1_ref,
    q_ref,
    k_ref,
    v_ref,
    pos_ref,
    tab_ref,
    rotor_ref,
    t_ref,
    p_ref,
    g_ref,
):
    mine = half_ref.shape[0]
    core = lax.axis_index("refl") % 2
    start = pl.multiple_of(core * mine, mine)
    rotors(rot_ref, shf_ref, rotor_ref)
    first_half = jnp.full((HALO, 128), core, jnp.int32) == 0
    halo = halo_ref[...].astype(F32)
    left = feat_ref[mine - HALO : mine, :].astype(F32)
    right = feat_ref[mine : mine + HALO, :].astype(F32)
    x_ref[0:HALO, :] = jnp.where(first_half, halo, left)
    x_ref[HALO : HALO + mine, :] = feat_ref[pl.ds(start, mine), :].astype(F32)
    x_ref[HALO + mine :, :] = jnp.where(first_half, right, halo)
    origin = lax.axis_index("atom") * feat_ref.shape[0] + start - HALO
    head_of = lax.broadcasted_iota(jnp.int32, (QWIN, 128), 1) // HEAD
    lane = lax.broadcasted_iota(jnp.int32, (1, KWIN), 1)
    scale = HEAD**-0.5 * math.log2(math.e)

    for layer in range(LAYERS):
        edge = 64 * layer
        size = x_ref.shape[0]
        part = min(size // 2, 640)
        from_ref, dest_ref = (x_ref, x1_ref) if layer == 0 else (x1_ref, x_ref)
        weights = jnp.concatenate(
            [wqkv_ref[g, layer, j] for j in range(3) for g in range(4)], axis=0
        )
        gain = gain_ref[layer : layer + 1, :]

        def project(i, _):
            r = pl.multiple_of(jnp.minimum(edge + i * part, size - edge - part), 64)
            xc = from_ref[pl.ds(r, part), :]
            cent = xc - jnp.mean(xc, axis=1, keepdims=True)
            var = jnp.mean(cent * cent, axis=1, keepdims=True)
            normed = (cent * lax.rsqrt(var + 1e-05) * gain).astype(BF)
            proj = dot(normed, weights, LANES).astype(BF)
            q_ref[pl.ds(r, part), :] = proj[:, 0:128]
            k_ref[pl.ds(r, part), :] = proj[:, 128:256]
            v_ref[pl.ds(r, part), :] = proj[:, 256:384]
            return 0

        lax.fori_loop(0, -(-(size - 2 * edge) // part), project, 0)
        w_out = wout_ref[layer]
        first = 64 * (layer + 1)
        rows = mine + 128 * (1 - layer)
        block = 64 * -(-rows // 128)
        ones = jnp.ones((KWIN, 128), BF)

        def attend(i, _):
            base = pl.multiple_of(jnp.minimum(first + i * block, first + rows - block), 64)
            scores = []
            for win in range(block // QWIN):
                r = base + win * QWIN
                qw = q_ref[pl.ds(pl.multiple_of(r, 32), QWIN), :]
                at = pl.multiple_of(r - BORDER, 16)
                kw = k_ref[pl.ds(at, KWIN), :]
                qm = jnp.concatenate(
                    [jnp.where(head_of == h, qw, jnp.zeros_like(qw)) for h in range(4)], axis=0
                )
                s = dot(qm, kw, LANES)
                place = lane + (origin + at)
                scores.append(jnp.where((place >= 0) & (place < natom), s, -1e30))
            tops = [jnp.max(s, axis=1, keepdims=True) for s in scores]
            heads = []
            for win in range(block // QWIN):
                at = pl.multiple_of(base + win * QWIN - BORDER, 16)
                vw = v_ref[pl.ds(at, KWIN), :]
                e = jnp.exp2((scores[win] - tops[win]) * scale).astype(BF)
                o = dot(e, jnp.concatenate([vw, ones], axis=1))
                o = o[:, 0:128] / o[:, 128:256]
                own = jnp.zeros((QWIN, 128), F32)
                for h in range(4):
                    own = jnp.where(head_of == h, o[QWIN * h : QWIN * h + QWIN], own)
                heads.append(own.astype(BF))
            y = dot(jnp.concatenate(heads, axis=0), w_out)
            dest_ref[pl.ds(base, block), :] = from_ref[pl.ds(base, block), :] + y
            return 0

        lax.fori_loop(0, -(-rows // block), attend, 0)

    pos_ref[...] = jnp.zeros_like(pos_ref)
    pos_ref[3:4, :] = power_ref[:, pl.ds(start, mine)]
    step = 256
    for i in range(mine // step):
        at = slice(i * step, (i + 1) * step)
        done = x_ref[HALO + i * step : HALO + (i + 1) * step, :].astype(BF)
        out_ref[pl.ds(start + i * step, step), :] = done
        half_ref[at, :] = done
        old = noisy_ref[:, pl.ds(start + i * step, step)]
        pos_ref[0:3, at] = old + 0.02 * dot(wcoord_ref[...], done, LANES)

    g_ref[...] = jnp.zeros_like(g_ref)
    chunks = mine // span
    prepare(pos_ref, tab_ref, TABLE_SPAN)

    def sums(i, _):
        s = i // chunks
        at = pl.multiple_of((i % chunks) * span, span)
        u = images(rot_ref, tab_ref, rotor_ref, t_ref, p_ref, s, at, span)
        u = split(u * pos_ref[3:4, pl.ds(at, span)], 2)
        g_ref[...] += dot(u, p_ref[...], LANES)
        return 0

    lax.fori_loop(0, nops * chunks, sums, 0)
    part_ref[:, 0:ROWS] = g_ref[0:32, :] + g_ref[32:64, :]
    quarter = mine // 4
    for i in range(4):
        part_ref[8 * i : 8 * i + 8, ROWS:] = pos_ref[:, i * quarter : (i + 1) * quarter]


def gather_kernel(norm, route_ref, own_ref, other_ref, miller_ref, pay_ref, pos_ref, re_ref, im_ref, f_ref):
    core = lax.axis_index("refl") % 2
    mine = pos_ref.shape[1] // 2
    quarter = mine // 4
    for i in range(4):
        rows = slice(8 * i, 8 * i + 8)
        pos_ref[:, pl.ds(pl.multiple_of(core * mine + i * quarter, quarter), quarter)] = own_ref[rows, ROWS:]
        pos_ref[:, pl.ds(pl.multiple_of((1 - core) * mine + i * quarter, quarter), quarter)] = other_ref[rows, ROWS:]
    grid = split(own_ref[:, 0:ROWS] + other_ref[:, 0:ROWS], 2)
    group = miller_ref.shape[1]
    wide = re_ref.shape[1]
    for c in range(group // wide):
        m = miller_ref[:, c * wide : (c + 1) * wide]
        fill_picks(re_ref, im_ref, m[1:2], m[2:3])
        yr = dot(grid, re_ref[...])
        yi = dot(grid, im_ref[...])
        yr = yr[0:32] + yr[32:64]
        yi = yi[0:32] + yi[32:64]
        uc, us = picks(m[0:1])
        fa = jnp.sum(uc * yr - us * yi, axis=0, keepdims=True) * norm
        fb = jnp.sum(uc * yi + us * yr, axis=0, keepdims=True) * norm
        for b in range(wide // 128):
            row = c * (wide // 128) + b
            f_ref[row : row + 1, :] = fa[:, b * 128 : (b + 1) * 128]
            f_ref[row + 8 : row + 9, :] = fb[:, b * 128 : (b + 1) * 128]

    both = f_ref[...]
    for e in range(pay_ref.shape[0]):
        blk = route_ref[0, e]
        at = pl.multiple_of(lax.shift_right_logical(blk, 1) * 128, 128)
        piece = pos_ref[:, pl.ds(at, 128)]
        odd = jnp.full(piece.shape, blk & 1, jnp.int32) == 1
        pay_ref[e, 0:16, :] = both
        pay_ref[e, 16:24, :] = jnp.where(odd, pltpu.roll(piece, 64, 1), piece)


def gradient_kernel(
    nrefl,
    norm,
    nops,
    span,
    rot_ref,
    shf_ref,
    recv_ref,
    miller_ref,
    obs_ref,
    wt_ref,
    amp_ref,
    grad_ref,
    pos_ref,
    tab_ref,
    rotor_ref,
    t_ref,
    p_ref,
    w_ref,
    re_ref,
    im_ref,
):
    shards = recv_ref.shape[0]
    rotors(rot_ref, shf_ref, rotor_ref)
    total = recv_ref[0, 0:16, :]
    for e in range(1, shards):
        total = total + recv_ref[e, 0:16, :]
    fa, fb = total[0:8], total[8:16]
    amp = jnp.sqrt(fa * fa + fb * fb + 1.0)
    slope = 2.0 * wt_ref[...] * (amp - obs_ref[...]) / (amp * math.sqrt(nrefl))
    amp_ref[...] = amp
    ga, gb = slope * fa, slope * fb
    left = lax.broadcasted_iota(jnp.int32, (8, 128), 1) < 64
    for j in range(shards // 2):
        other = pltpu.roll(recv_ref[2 * j + 1, 16:24, :], 64, 1)
        pos_ref[:, 128 * j : 128 * j + 128] = jnp.where(left, recv_ref[2 * j, 16:24, :], other)

    group = miller_ref.shape[1]
    wide = re_ref.shape[1]
    rows = wide // 128
    for c in range(group // wide):
        m = miller_ref[:, c * wide : (c + 1) * wide]
        fill_picks(re_ref, im_ref, m[1:2], m[2:3])
        uc, us = picks(m[0:1])
        a = jnp.concatenate([ga[c * rows + b : c * rows + b + 1] for b in range(rows)], axis=1)
        b = jnp.concatenate([gb[c * rows + b : c * rows + b + 1] for b in range(rows)], axis=1)
        real = b * uc - a * us
        imag = -(a * uc + b * us)
        mf = m.astype(F32)
        real = jnp.concatenate([mf[k : k + 1] * real for k in range(3)], axis=0).astype(BF)
        imag = jnp.concatenate([mf[k : k + 1] * imag for k in range(3)], axis=0).astype(BF)
        part = dot(real, re_ref[...], LANES) + dot(imag, im_ref[...], LANES)
        w_ref[...] = part if c == 0 else w_ref[...] + part
    coef = w_ref[...].astype(BF)
    local = pos_ref.shape[1]
    grad_ref[...] = jnp.zeros_like(grad_ref)
    chunks = local // span
    factor = 2.0 * math.pi * norm
    prepare(pos_ref, tab_ref, TABLE_SPAN)

    def slopes(i, _):
        s = i // chunks
        at = pl.multiple_of((i % chunks) * span, span)
        u = images(rot_ref, tab_ref, rotor_ref, t_ref, p_ref, s, at, span)
        t = dot(coef, p_ref[...])
        scale = pos_ref[3:4, pl.ds(at, span)] * factor
        g = [jnp.sum(u * t[32 * k : 32 * k + 32], axis=0, keepdims=True) * scale for k in range(3)]
        for c in range(3):
            r = rot_ref[s, 0, c].astype(F32) * g[0]
            r = r + rot_ref[s, 1, c].astype(F32) * g[1]
            r = r + rot_ref[s, 2, c].astype(F32) * g[2]
            grad_ref[c : c + 1, pl.ds(at, span)] += r
        return 0

    lax.fori_loop(0, nops * chunks, slopes, 0)


def body(
    features,
    ln_gain,
    w_qkv,
    w_out,
    w_coord,
    noisy_coords,
    scatter_power,
    route,
    miller,
    rotations,
    shifts,
    observed,
    obs_weight,
):
    shards = lax.axis_size("atom")
    rank = lax.axis_index("atom")
    local = features.shape[0]
    natom = local * shards
    group = miller.shape[1]
    nops = rotations.shape[0]
    nrefl = group * lax.axis_size("refl")
    norm = 1.0 / math.sqrt(nops * natom)
    span = SPAN
    wide = 256
    smem = pl.BlockSpec(memory_space=pltpu.SMEM)
    vmem = pl.BlockSpec(memory_space=pltpu.VMEM)

    core = lax.axis_index("refl") % 2
    mine = local // 2
    ahead = [(g * shards + i, g * shards + i + 1) for g in (0, 2) for i in range(shards - 1)]
    back = [(g * shards + i + 1, g * shards + i) for g in (1, 3) for i in range(shards - 1)]
    edge = lax.dynamic_slice_in_dim(features, (1 - core) * (local - HALO), HALO, 0)
    halo = lax.ppermute(edge, ("refl", "atom"), ahead + back)
    weights = lax.all_gather(w_qkv.transpose(0, 1, 3, 2), "refl")
    params = pltpu.CompilerParams(vmem_limit_bytes=60 * 1024 * 1024)
    swap = [(0, 1), (1, 0), (2, 3), (3, 2)]
    cross = [(0, 2), (2, 0), (1, 3), (3, 1)]
    tables = [
        pltpu.VMEM((3, 80, mine), F32),
        pltpu.VMEM((nops, 2, 96, 128), F32),
        pltpu.VMEM((32, span), F32),
        pltpu.VMEM((ROWS, span), BF),
    ]
    picked = [pltpu.VMEM((ROWS, wide), BF), pltpu.VMEM((ROWS, wide), BF)]
    atoms, half, part = pl.pallas_call(
        functools.partial(attend_kernel, natom, nops, span),
        out_shape=(
            jax.ShapeDtypeStruct((local, 128), BF),
            jax.ShapeDtypeStruct((mine, 128), BF),
            jax.ShapeDtypeStruct((32, ROWS + mine // 4), F32),
        ),
        in_specs=[smem] * 2 + [vmem] * 8,
        out_specs=(vmem,) * 3,
        scratch_shapes=[
            pltpu.VMEM((mine + 2 * HALO, 128), F32),
            pltpu.VMEM((mine + 2 * HALO, 128), F32),
            pltpu.VMEM((mine + 2 * HALO, 128), BF),
            pltpu.VMEM((mine + 2 * HALO, 128), BF),
            pltpu.VMEM((mine + 2 * HALO, 128), BF),
            pltpu.VMEM((8, mine), F32),
            *tables,
            pltpu.VMEM((64, ROWS), F32),
        ],
        compiler_params=params,
        name="attend",
    )(
        rotations,
        shifts,
        features,
        halo,
        weights,
        w_out,
        ln_gain,
        w_coord,
        noisy_coords,
        scatter_power[None, :],
    )
    payload = pl.pallas_call(
        functools.partial(gather_kernel, norm),
        out_shape=jax.ShapeDtypeStruct((shards, 24, 128), F32),
        in_specs=[smem] + [vmem] * 3,
        out_specs=vmem,
        scratch_shapes=[pltpu.VMEM((8, local), F32), *picked, pltpu.VMEM((16, 128), F32)],
        compiler_params=params,
        name="gather",
    )(route, part, lax.ppermute(part, "refl", swap), miller)
    atom_out = lax.dynamic_update_slice_in_dim(
        atoms, lax.ppermute(half, "refl", swap), (1 - core) * mine, 0
    )
    recv = lax.all_to_all(payload, "atom", split_axis=0, concat_axis=0, tiled=True)
    amp, grad = pl.pallas_call(
        functools.partial(gradient_kernel, nrefl, norm, nops, span),
        out_shape=(
            jax.ShapeDtypeStruct((8, 128), F32),
            jax.ShapeDtypeStruct((3, local), F32),
        ),
        in_specs=[smem] * 2 + [vmem] * 4,
        out_specs=(vmem, vmem),
        scratch_shapes=[
            pltpu.VMEM((8, local), F32),
            pltpu.VMEM((3, 80, local), F32),
            *tables[1:],
            pltpu.VMEM((96, ROWS), F32),
            *picked,
        ],
        compiler_params=params,
        name="gradient",
    )(rotations, shifts, recv, miller, observed.reshape(8, 128), obs_weight.reshape(8, 128))
    grad = grad + lax.ppermute(grad, "refl", swap)
    grad = grad + lax.ppermute(grad, "refl", cross)
    share = group // shards
    amplitude = lax.dynamic_slice_in_dim(amp.reshape(group), rank * share, share, 0)
    return (atom_out, amplitude, grad)


def solution(mesh):
    placed = (
        P("atom", None),
        P(),
        P(None, None, None, "refl"),
        P(),
        P(),
        P(None, "atom"),
        P("atom"),
        P("atom", None),
        P(None, "refl"),
        P(),
        P(),
        P("refl"),
        P("refl"),
    )
    return jax.shard_map(
        body,
        mesh=mesh,
        in_specs=placed,
        out_specs=(P("atom", None), P(("refl", "atom")), P(None, "atom")),
        check_vma=False,
    )
```

time: 129 us -> 65.2 us (0.51)
  Pallas kernels: 80.5 us -> 19.5 us
  blocking collectives: 30.8 us -> 7.55 us
  waiting for transfers between devices: 2.68 us -> 14.7 us
  starting transfers between devices: 8.81 us -> 16.2 us
  local copies, waits for them, and re-layouts: 3.33 us -> 4.71 us
    pallas_call x1 -> x2, Pallas kernels: 71.1 us -> 13 us  [the longest x1 10.6 us: body(): pl.pallas_call(functools.partial(attend_kernel, natom, nops, span), out_s...]
    all_to_all x1 -> x0, blocking collectives: 23.2 us -> none  [body(): lax.all_to_all(payload, 'atom', split_axis=0, concat_axis=0, tiled=True)]
    all_to_all x0 -> x1, waiting for transfers between devices: none -> 11.2 us  [body(): lax.all_to_all(payload, 'atom', split_axis=0, concat_axis=0, tiled=True)]
    all_to_all x0 -> x1, starting transfers between devices: none -> 8.81 us  [body(): lax.all_to_all(payload, 'atom', split_axis=0, concat_axis=0, tiled=True)]
    pallas_call x1, Pallas kernels: 9.37 us -> 6.49 us  [body(): pl.pallas_call(functools.partial(gradient_kernel, nrefl, norm, nops, span...]
    unnamed x9 -> x17, local copies, waits for them, and re-layouts: 0.62 us -> 2.64 us
    ppermute x4 -> x5, starting transfers between devices: 8.81 us -> 7.35 us  [the longest x1 3.58 us: body(): halo = lax.ppermute(edge, ('refl', 'atom'), ahead + back)]
    ppermute x4 -> x5, waiting for transfers between devices: 2.68 us -> 3.51 us  [the longest x1 1.42 us: body(): grad = grad + lax.ppermute(grad, 'refl', swap)]
  transfers between devices with their start and end apart: 4 -> 6, of which waited for: 2 -> 4; matrix products, arithmetic and copies ran while one was open for 1% -> 4% of each run, Pallas kernels for 0% -> 10%
where the time goes in v2:
time: 65.2 us; the launch traced here: 64.7 us
  Pallas kernels  19.5 us (30%)
  starting transfers between devices  16.2 us (25%)
  waiting for transfers between devices  14.7 us (23%)
  blocking collectives  7.55 us (12%)
  local copies, waits for them, and re-layouts  4.71 us (7%)
  other arithmetic  1.39 us (2%)
  between operations  0.73 us (1%)
    all_to_all x1, waiting for transfers between devices, body(): lax.all_to_all(payload, 'atom', split_axis=0, concat_axis=0, tiled=True)  11.2 us
    pallas_call x1, Pallas kernels, body(): pl.pallas_call(functools.partial(attend_kernel, natom, nops, span), out_s...  10.6 us
    all_to_all x1, starting transfers between devices, body(): lax.all_to_all(payload, 'atom', split_axis=0, concat_axis=0, tiled=True)  8.81 us
    all_gather x1, blocking collectives, body(): weights = lax.all_gather(w_qkv.transpose(0, 1, 3, 2), 'refl')  7.55 us
    pallas_call x1, Pallas kernels, body(): pl.pallas_call(functools.partial(gradient_kernel, nrefl, norm, nops, span...  6.49 us
    ppermute x1, starting transfers between devices, body(): halo = lax.ppermute(edge, ('refl', 'atom'), ahead + back)  3.58 us
    ppermute x1, starting transfers between devices, body(): grad = grad + lax.ppermute(grad, 'refl', cross)  3.28 us
    unnamed x17, local copies, waits for them, and re-layouts  2.64 us
  transfers between devices with their start and end apart: 6, of which 4 were waited for; matrix products, arithmetic and copies ran while one was open for 4% of the time, Pallas kernels for 10%

profile of v2, /device:TPU:0, one launch (start us, length us, event | category | flops | bytes accessed | tf_op | source)
XLA Modules:
  0.0 64.7 jit_solution(13742899695180504180)
XLA Ops:
  0.6 0.0 copy-start.2
  0.7 0.8 %constant_dynamic-slice_fusion = bf16[128,128]{1,0:T(8,128)(2,1)S(1)} fusion(bf16[2048,128]{1,0:T(8,128)(2,1)} %feat_ref.1, s32[]{:T(128)S(6)} %select_n.17), kind=kLoop, calls=%fused_computation.1 | loop fusion | bytes 65540 | tf_op jit(solution)/shard_map/dynamic_slice | solution.py:467
  1.4 3.6 %collective-permute-start = (bf16[128,128]{1,0:T(8,128)(2,1)S(1)}, bf16[128,128]{1,0:T(8,128)(2,1)S(1)}, u32[]{:S(2)}, u32[]{:S(2)}) collective-permute-start(bf16[128,128]{1,0:T(8,128)(2,1)S(1)} %constant_dynamic-slice_fusion), channel_id=1, source_target_pairs={{0,1},{1,2},{2,3},{3,4},{4,5},{5,6},{6,7},{7,8},{8,9},{9,10},{10,1... | collective-permute-start | bytes 98312 | tf_op jit(solution)/shard_map/ppermute | solution.py:468
  5.0 0.0 copy-done.2
  5.0 0.0 copy-start.4
  5.0 7.6 %all-gather = bf16[8,3,32,128]{3,2,1,0:T(8,128)(2,1)} all-gather(bf16[2,3,32,128]{3,2,1,0:T(8,128)(2,1)S(1)} %bitcast.7), channel_id=2, replica_groups=mesh['refl'=4,'atom'=32] {'refl'}, dimensions={0}, use_global_device_ids=true | all-gather | bytes 245760 | tf_op jit(solution)/shard_map/all_gather | solution.py:469
  12.6 0.0 copy-done.4
  12.6 0.6 copy.18.rot_ref
  13.2 0.0 collective-permute-done.halo_ref
  13.2 0.6 copy-done.3
  13.8 10.6 %attend.1 = (bf16[2048,128]{1,0:T(8,128)(2,1)}, bf16[1024,128]{1,0:T(8,128)(2,1)}, f32[32,896]{1,0:T(8,128)}) custom-call(s32[4,3,3]{2,1,0:T(4,128)} %copy.18.rot_ref, f32[4,3]{1,0:T(4,128)} %shf_ref.3, bf16[2048,128]{1,0:T(8,128)(2,1)} %feat_ref.1, bf16[128,128]{1,0:T(8,128)(2,1)} %copy-done.3, bf16[4,2,3,32,128]{4,3,2,1,0:T(8,128)(2,1)} %bitcast.6, ...), custom_call_target="tpu_custom_call" | custom-call | tf_op jit(solution)/shard_map/attend/pallas_call | solution.py:480
  24.4 0.3 collective-permute-start.2
  24.7 1.2 %collective-permute-done.2.other_ref = f32[32,896]{1,0:T(8,128)S(1)} collective-permute-done((f32[32,896]{1,0:T(8,128)}, f32[32,896]{1,0:T(8,128)S(1)}, u32[]{:S(2)}, u32[]{:S(2)}) %collective-permute-start.2) | collective-permute-done | bytes 114720 | tf_op jit(solution)/shard_map/ppermute | solution.py:521
  26.0 0.6 copy-done.1
  26.6 2.4 %gather.1 = f32[32,24,128]{2,1,0:T(8,128)} custom-call(s32[1,32]{1,0:T(1,128)} %route_ref.1, f32[32,896]{1,0:T(8,128)} %get-tuple-element.10.own_ref, f32[32,896]{1,0:T(8,128)} %copy-done.1, s32[3,1024]{1,0:T(4,128)} %miller_ref.3), custom_call_target="tpu_custom_call" | custom-call | tf_op jit(solution)/shard_map/gather/pallas_call | solution.py:513
  29.0 8.8 %all-to-all-start = ((f32[32,24,128]{2,1,0:T(8,128)}), f32[32,24,128]{2,1,0:T(8,128)S(1)}, u32[]{:S(2)}, u32[]{:S(2)}) async-start(f32[32,24,128]{2,1,0:T(8,128)} %gather.1), calls=%async_computation | async-start | bytes 786432 | tf_op jit(solution)/shard_map/all_to_all | solution.py:525
  37.8 0.0 copy-done.7
  37.8 0.2 collective-permute-start.1
  38.0 11.2 %all-to-all-done.recv_ref = f32[32,24,128]{2,1,0:T(8,128)S(1)} async-done(((f32[32,24,128]{2,1,0:T(8,128)}), f32[32,24,128]{2,1,0:T(8,128)S(1)}, u32[]{:S(2)}, u32[]{:S(2)}) %all-to-all-start) | async-done | bytes 393248 | tf_op jit(solution)/shard_map/all_to_all | solution.py:525
  49.1 0.8 %copy-done = f32[32,24,128]{2,1,0:T(8,128)} copy-done((f32[32,24,128]{2,1,0:T(8,128)}, f32[32,24,128]{2,1,0:T(8,128)S(1)}, u32[]{:S(2)}) %copy-start) | copy-done | bytes 393240
  49.9 6.5 %gradient.1 = (f32[8,128]{1,0:T(8,128)}, f32[3,2048]{1,0:T(4,128)}) custom-call(s32[4,3,3]{2,1,0:T(4,128)} %copy.18.rot_ref, f32[4,3]{1,0:T(4,128)} %shf_ref.3, f32[32,24,128]{2,1,0:T(8,128)} %copy-done, s32[3,1024]{1,0:T(4,128)} %miller_ref.3, f32[8,128]{1,0:T(8,128)} %bitcast.9, f32[8,128]{1,0:T(8,128)} %bitcast.10), custom_call_target="tpu_custom_call" | custom-call | tf_op jit(solution)/shard_map/gradient/pallas_call | solution.py:526
  56.4 0.0 collective-permute-start.3
  56.4 1.4 %collective-permute-done.3 = f32[3,2048]{1,0:T(4,128)S(1)} collective-permute-done((f32[3,2048]{1,0:T(4,128)}, f32[3,2048]{1,0:T(4,128)S(1)}, u32[]{:S(2)}, u32[]{:S(2)}) %collective-permute-start.3) | collective-permute-done | bytes 24608 | tf_op jit(solution)/shard_map/ppermute | solution.py:544
  57.8 0.8 %add.23 = f32[3,2048]{1,0:T(4,128)S(1)} add(f32[3,2048]{1,0:T(4,128)} %get-tuple-element.12, f32[3,2048]{1,0:T(4,128)S(1)} %collective-permute-done.3) | non-fusion elementwise | flops 6144 | bytes 73728 | tf_op jit(solution)/shard_map/add | solution.py:544
  58.6 3.3 %collective-permute-start.4 = (f32[3,2048]{1,0:T(4,128)S(1)}, f32[3,2048]{1,0:T(4,128)S(1)}, u32[]{:S(2)}, u32[]{:S(2)}) collective-permute-start(f32[3,2048]{1,0:T(4,128)S(1)} %add.23), channel_id=1, source_target_pairs={{0,64},{64,0},{32,96},{96,32},{1,65},{65,1},{33,97},{97,33},{2,66}... | collective-permute-start | bytes 73736 | tf_op jit(solution)/shard_map/ppermute | solution.py:545
  61.9 0.0 collective-permute-done.1
  61.9 0.0 copy-done.5
  61.9 0.0 copy-start.6
  61.9 1.3 %dynamic_slice.7 = f32[32]{0:T(128)} dynamic-slice(f32[1024]{0:T(1024)} %bitcast.11, s32[]{:T(128)S(6)} %select_n.19), dynamic_slice_sizes={32} | dynamic-slice | bytes 260 | tf_op jit(solution)/shard_map/dynamic_slice | solution.py:547
  63.2 0.9 %collective-permute-done.4 = f32[3,2048]{1,0:T(4,128)S(1)} collective-permute-done((f32[3,2048]{1,0:T(4,128)S(1)}, f32[3,2048]{1,0:T(4,128)S(1)}, u32[]{:S(2)}, u32[]{:S(2)}) %collective-permute-start.4) | collective-permute-done | bytes 24608 | tf_op jit(solution)/shard_map/ppermute | solution.py:545
  64.1 0.6 add.24
  64.7 0.0 copy-done.6
  (6 shorter events, 0.0 us)
Async XLA Ops:
  0.6 4.4 %copy-start.2 = (bf16[2,3,128,32]{2,3,1,0:T(8,128)(2,1)S(1)}, bf16[2,3,128,32]{2,3,1,0:T(8,128)(2,1)}, u32[]{:S(2)}) copy-start(bf16[2,3,128,32]{2,3,1,0:T(8,128)(2,1)} %param.15) | copy-start | bytes 147460
  1.4 11.8 %collective-permute-start = (bf16[128,128]{1,0:T(8,128)(2,1)S(1)}, bf16[128,128]{1,0:T(8,128)(2,1)S(1)}, u32[]{:S(2)}, u32[]{:S(2)}) collective-permute-start(bf16[128,128]{1,0:T(8,128)(2,1)S(1)} %constant_dynamic-slice_fusion), channel_id=1, source_target_pairs={{0,1},{1,2},{2,3},{3,4},{4,5},{5,6},{6,7},{7,8},{8,9},{9,10},{10,1... | collective-permute-start | bytes 98312 | tf_op jit(solution)/shard_map/ppermute | solution.py:468
  5.0 7.6 %copy-start.4 = (s32[4,3,3]{2,0,1:T(4,128)S(1)}, s32[4,3,3]{2,0,1:T(4,128)}, u32[]{:S(2)}) copy-start(s32[4,3,3]{2,0,1:T(4,128)} %param.22) | copy-start | bytes 436
  13.2 0.6 copy-start.3
  24.4 1.5 %collective-permute-start.2 = (f32[32,896]{1,0:T(8,128)}, f32[32,896]{1,0:T(8,128)S(1)}, u32[]{:S(2)}, u32[]{:S(2)}) collective-permute-start(f32[32,896]{1,0:T(8,128)} %get-tuple-element.10.own_ref), channel_id=1, source_target_pairs={{0,32},{32,0},{64,96},{96,64},{1,33},{33,1},{65,97},{97,65},{2,34}... | collective-permute-start | bytes 344072 | tf_op jit(solution)/shard_map/ppermute | solution.py:521
  26.0 0.6 copy-start.1
  29.0 8.8 %copy-start.7 = (bf16[1024,128]{1,0:T(8,128)(2,1)S(1)}, bf16[1024,128]{1,0:T(8,128)(2,1)}, u32[]{:S(2)}) copy-start(bf16[1024,128]{1,0:T(8,128)(2,1)} %get-tuple-element.9) | copy-start | bytes 786436
  29.0 32.9 %copy-start.5 = (bf16[2048,128]{1,0:T(8,128)(2,1)S(1)}, bf16[2048,128]{1,0:T(8,128)(2,1)}, u32[]{:S(2)}) copy-start(bf16[2048,128]{1,0:T(8,128)(2,1)} %get-tuple-element.8) | copy-start | bytes 1572868
  29.0 20.2 %all-to-all-start = ((f32[32,24,128]{2,1,0:T(8,128)}), f32[32,24,128]{2,1,0:T(8,128)S(1)}, u32[]{:S(2)}, u32[]{:S(2)}) async-start(f32[32,24,128]{2,1,0:T(8,128)} %gather.1), calls=%async_computation | async-start | bytes 786432 | tf_op jit(solution)/shard_map/all_to_all | solution.py:525
  37.8 24.0 %collective-permute-start.1 = (bf16[1024,128]{1,0:T(8,128)(2,1)S(1)}, bf16[1024,128]{1,0:T(8,128)(2,1)S(1)}, u32[]{:S(2)}, u32[]{:S(2)}) collective-permute-start(bf16[1024,128]{1,0:T(8,128)(2,1)S(1)} %copy-done.7), channel_id=1, source_target_pairs={{0,32},{32,0},{64,96},{96,64},{1,33},{33,1},{65,97},{97,65},{2,34}... | collective-permute-start | bytes 786440 | tf_op jit(solution)/shard_map/ppermute | solution.py:523
  49.1 0.8 %copy-start = (f32[32,24,128]{2,1,0:T(8,128)}, f32[32,24,128]{2,1,0:T(8,128)S(1)}, u32[]{:S(2)}) copy-start(f32[32,24,128]{2,1,0:T(8,128)S(1)} %all-to-all-done.recv_ref) | copy-start | bytes 1179652
  56.4 1.4 %collective-permute-start.3 = (f32[3,2048]{1,0:T(4,128)}, f32[3,2048]{1,0:T(4,128)S(1)}, u32[]{:S(2)}, u32[]{:S(2)}) collective-permute-start(f32[3,2048]{1,0:T(4,128)} %get-tuple-element.12), channel_id=1, source_target_pairs={{0,32},{32,0},{64,96},{96,64},{1,33},{33,1},{65,97},{97,65},{2,34}... | collective-permute-start | bytes 73736 | tf_op jit(solution)/shard_map/ppermute | solution.py:544
  58.6 5.5 %collective-permute-start.4 = (f32[3,2048]{1,0:T(4,128)S(1)}, f32[3,2048]{1,0:T(4,128)S(1)}, u32[]{:S(2)}, u32[]{:S(2)}) collective-permute-start(f32[3,2048]{1,0:T(4,128)S(1)} %add.23), channel_id=1, source_target_pairs={{0,64},{64,0},{32,96},{96,32},{1,65},{65,1},{33,97},{97,33},{2,66}... | collective-permute-start | bytes 73736 | tf_op jit(solution)/shard_map/ppermute | solution.py:545
  61.9 2.8 %copy-start.6 = (bf16[2048,128]{1,0:T(8,128)(2,1)}, bf16[2048,128]{1,0:T(8,128)(2,1)S(1)}, u32[]{:S(2)}) copy-start(bf16[2048,128]{1,0:T(8,128)(2,1)S(1)} %constant_dynamic-update-slice_fusion) | copy-start | bytes 1572868

commit v3 on v2

--- a/solution.py
+++ b/solution.py
@@ -83,7 +83,7 @@
     for s in range(nops):
         for k in range(3):
             here = lane == 3 * s + k
-            whole = rot_ref[s, k, 0] + rot_ref[s, k, 1] + rot_ref[s, k, 2]
+            whole = rot_ref[k, s, 0] + rot_ref[k, s, 1] + rot_ref[k, s, 2]
             turn = jnp.where(here, shf_ref[s, k], turn)
             sign = jnp.where(here, whole.astype(F32), sign)
     i = lax.broadcasted_iota(jnp.int32, (32, 1), 0)
@@ -109,7 +109,7 @@
 
 def images(rot_ref, tab_ref, rotor_ref, v_ref, p_ref, s, at, span):
     def table(k, r, size):
-        axis = jnp.abs(rot_ref[s, k, 1]) + 2 * jnp.abs(rot_ref[s, k, 2])
+        axis = jnp.abs(rot_ref[k, s, 1]) + 2 * jnp.abs(rot_ref[k, s, 2])
         return tab_ref[axis, r : r + size, pl.ds(at, span)]
 
     def factor(kind, r, size):
@@ -131,9 +131,13 @@
     def row(j):
         return v_ref[ORDER[j] : ORDER[j] + 1, :]
 
+    def spread(j):
+        return jnp.broadcast_to(row(j), (24, span))
+
+    w2 = jnp.concatenate([w, w], axis=0).astype(BF)
     for j in range(TOP):
-        pair = jnp.concatenate([row(2 * j) * w, row(2 * j + 1) * w], axis=0)
-        p_ref[48 * j : 48 * j + 48, :] = pair.astype(BF)
+        pair = jnp.concatenate([spread(2 * j), spread(2 * j + 1)], axis=0).astype(BF)
+        p_ref[48 * j : 48 * j + 48, :] = pair * w2
     pad = jnp.zeros((8, span), F32)
     p_ref[576:640, :] = jnp.concatenate([row(24) * w, v * last, pad], axis=0).astype(BF)
     return both(0)
@@ -209,9 +213,11 @@
     tab_ref,
     rotor_ref,
     t_ref,
-    p_ref,
+    p0_ref,
+    p1_ref,
     g_ref,
 ):
+    p_refs = (p0_ref, p1_ref)
     mine = half_ref.shape[0]
     core = lax.axis_index("refl") % 2
     start = pl.multiple_of(core * mine, mine)
@@ -305,14 +311,17 @@
     prepare(pos_ref, tab_ref, TABLE_SPAN)
 
     def sums(i, _):
-        s = i // chunks
-        at = pl.multiple_of((i % chunks) * span, span)
-        u = images(rot_ref, tab_ref, rotor_ref, t_ref, p_ref, s, at, span)
-        u = split(u * pos_ref[3:4, pl.ds(at, span)], 2)
-        g_ref[...] += dot(u, p_ref[...], LANES)
+        at = pl.multiple_of(i * span, span)
+        power = pos_ref[3:4, pl.ds(at, span)]
+        total = g_ref[...]
+        for s in range(nops):
+            p_ref = p_refs[s % 2]
+            u = images(rot_ref, tab_ref, rotor_ref, t_ref.at[s % 2], p_ref, s, at, span)
+            total = total + dot(split(u * power, 2), p_ref[...], LANES)
+        g_ref[...] = total
         return 0
 
-    lax.fori_loop(0, nops * chunks, sums, 0)
+    lax.fori_loop(0, chunks, sums, 0)
     part_ref[:, 0:ROWS] = g_ref[0:32, :] + g_ref[32:64, :]
     quarter = mine // 4
     for i in range(4):
@@ -372,11 +381,13 @@
     tab_ref,
     rotor_ref,
     t_ref,
-    p_ref,
+    p0_ref,
+    p1_ref,
     w_ref,
     re_ref,
     im_ref,
 ):
+    p_refs = (p0_ref, p1_ref)
     shards = recv_ref.shape[0]
     rotors(rot_ref, shf_ref, rotor_ref)
     total = recv_ref[0, 0:16, :]
@@ -410,26 +421,27 @@
         w_ref[...] = part if c == 0 else w_ref[...] + part
     coef = w_ref[...].astype(BF)
     local = pos_ref.shape[1]
-    grad_ref[...] = jnp.zeros_like(grad_ref)
     chunks = local // span
     factor = 2.0 * math.pi * norm
     prepare(pos_ref, tab_ref, TABLE_SPAN)
 
     def slopes(i, _):
-        s = i // chunks
-        at = pl.multiple_of((i % chunks) * span, span)
-        u = images(rot_ref, tab_ref, rotor_ref, t_ref, p_ref, s, at, span)
-        t = dot(coef, p_ref[...])
+        at = pl.multiple_of(i * span, span)
         scale = pos_ref[3:4, pl.ds(at, span)] * factor
-        g = [jnp.sum(u * t[32 * k : 32 * k + 32], axis=0, keepdims=True) * scale for k in range(3)]
+        total = [jnp.zeros((1, span), F32)] * 3
+        for s in range(nops):
+            p_ref = p_refs[s % 2]
+            u = images(rot_ref, tab_ref, rotor_ref, t_ref.at[s % 2], p_ref, s, at, span)
+            t = dot(coef, p_ref[...])
+            g = [jnp.sum(u * t[32 * k : 32 * k + 32], axis=0, keepdims=True) for k in range(3)]
+            for c in range(3):
+                for k in range(3):
+                    total[c] = total[c] + rot_ref[k, s, c].astype(F32) * g[k]
         for c in range(3):
-            r = rot_ref[s, 0, c].astype(F32) * g[0]
-            r = r + rot_ref[s, 1, c].astype(F32) * g[1]
-            r = r + rot_ref[s, 2, c].astype(F32) * g[2]
-            grad_ref[c : c + 1, pl.ds(at, span)] += r
+            grad_ref[c : c + 1, pl.ds(at, span)] = total[c] * scale
         return 0
 
-    lax.fori_loop(0, nops * chunks, slopes, 0)
+    lax.fori_loop(0, chunks, slopes, 0)
 
 
 def body(
@@ -467,13 +479,15 @@
     edge = lax.dynamic_slice_in_dim(features, (1 - core) * (local - HALO), HALO, 0)
     halo = lax.ppermute(edge, ("refl", "atom"), ahead + back)
     weights = lax.all_gather(w_qkv.transpose(0, 1, 3, 2), "refl")
-    params = pltpu.CompilerParams(vmem_limit_bytes=60 * 1024 * 1024)
+    turns = rotations.transpose(1, 0, 2)
+    params = pltpu.CompilerParams(vmem_limit_bytes=24 * 1024 * 1024)
     swap = [(0, 1), (1, 0), (2, 3), (3, 2)]
     cross = [(0, 2), (2, 0), (1, 3), (3, 1)]
     tables = [
         pltpu.VMEM((3, 80, mine), F32),
         pltpu.VMEM((nops, 2, 96, 128), F32),
-        pltpu.VMEM((32, span), F32),
+        pltpu.VMEM((2, 32, span), F32),
+        pltpu.VMEM((ROWS, span), BF),
         pltpu.VMEM((ROWS, span), BF),
     ]
     picked = [pltpu.VMEM((ROWS, wide), BF), pltpu.VMEM((ROWS, wide), BF)]
@@ -499,7 +513,7 @@
         compiler_params=params,
         name="attend",
     )(
-        rotations,
+        turns,
         shifts,
         features,
         halo,
@@ -540,7 +554,7 @@
         ],
         compiler_params=params,
         name="gradient",
-    )(rotations, shifts, recv, miller, observed.reshape(8, 128), obs_weight.reshape(8, 128))
+    )(turns, shifts, recv, miller, observed.reshape(8, 128), obs_weight.reshape(8, 128))
     grad = grad + lax.ppermute(grad, "refl", swap)
     grad = grad + lax.ppermute(grad, "refl", cross)
     share = group // shards

time: 65.2 us -> 59.6 us (0.914)
  Pallas kernels: 19.5 us -> 16.2 us
  local copies, waits for them, and re-layouts: 4.71 us -> 3.24 us
  other arithmetic: 1.39 us -> 0.63 us
    pallas_call x1, Pallas kernels: 6.49 us -> 4.7 us  [body(): pl.pallas_call(functools.partial(gradient_kernel, nrefl, norm, nops, span...]
    pallas_call x1, Pallas kernels: 10.6 us -> 9.55 us  [body(): pl.pallas_call(functools.partial(attend_kernel, natom, nops, span), out_s...]
    unnamed x17 -> x30, local copies, waits for them, and re-layouts: 2.64 us -> 1.76 us
    add x1, other arithmetic: 0.77 us -> 0.01 us  [body(): grad = grad + lax.ppermute(grad, 'refl', swap)]
  transfers between devices with their start and end apart: 6 -> 6, of which waited for: 4 -> 4; matrix products, arithmetic and copies ran while one was open for 4% -> 1% of each run, Pallas kernels for 10% -> 8%
where the time goes in v3:
time: 59.6 us; the launch traced here: 59.2 us
  starting transfers between devices  16.2 us (27%)
  Pallas kernels  16.2 us (27%)
  waiting for transfers between devices  14.8 us (25%)
  blocking collectives  7.23 us (12%)
  local copies, waits for them, and re-layouts  3.24 us (5%)
  between operations  0.82 us (1%)
  other arithmetic  0.63 us (1%)
    all_to_all x1, waiting for transfers between devices, body(): lax.all_to_all(payload, 'atom', split_axis=0, concat_axis=0, tiled=True)  11.2 us
    pallas_call x1, Pallas kernels, body(): pl.pallas_call(functools.partial(attend_kernel, natom, nops, span), out_s...  9.55 us
    all_to_all x1, starting transfers between devices, body(): lax.all_to_all(payload, 'atom', split_axis=0, concat_axis=0, tiled=True)  8.82 us
    all_gather x1, blocking collectives, body(): weights = lax.all_gather(w_qkv.transpose(0, 1, 3, 2), 'refl')  7.23 us
    pallas_call x1, Pallas kernels, body(): pl.pallas_call(functools.partial(gradient_kernel, nrefl, norm, nops, span...  4.7 us
    ppermute x1, starting transfers between devices, body(): halo = lax.ppermute(edge, ('refl', 'atom'), ahead + back)  3.58 us
    ppermute x1, starting transfers between devices, body(): grad = grad + lax.ppermute(grad, 'refl', cross)  3.28 us
    pallas_call x1, Pallas kernels, body(): pl.pallas_call(functools.partial(gather_kernel, norm), out_shape=jax.Shap...  1.96 us
  transfers between devices with their start and end apart: 6, of which 4 were waited for; matrix products, arithmetic and copies ran while one was open for 1% of the time, Pallas kernels for 8%

profile of v3, /device:TPU:0, one launch (start us, length us, event | category | flops | bytes accessed | tf_op | source)
XLA Modules:
  0.0 59.2 jit_solution(844934284959096192)
XLA Ops:
  0.7 0.8 %constant_dynamic-slice_fusion = bf16[128,128]{1,0:T(8,128)(2,1)S(1)} fusion(bf16[2048,128]{1,0:T(8,128)(2,1)} %feat_ref.1, s32[]{:T(128)S(6)} %select_n.17), kind=kLoop, calls=%fused_computation.1 | loop fusion | bytes 65540 | tf_op jit(solution)/shard_map/dynamic_slice | solution.py:479
  1.4 3.6 %collective-permute-start = (bf16[128,128]{1,0:T(8,128)(2,1)S(1)}, bf16[128,128]{1,0:T(8,128)(2,1)S(1)}, u32[]{:S(2)}, u32[]{:S(2)}) collective-permute-start(bf16[128,128]{1,0:T(8,128)(2,1)S(1)} %constant_dynamic-slice_fusion), channel_id=1, source_target_pairs={{0,1},{1,2},{2,3},{3,4},{4,5},{5,6},{6,7},{7,8},{8,9},{9,10},{10,1... | collective-permute-start | bytes 98312 | tf_op jit(solution)/shard_map/ppermute | solution.py:480
  5.0 0.0 copy-start.1
  5.0 0.0 copy-start.3
  5.0 0.0 copy-start.4
  5.1 0.0 copy-start.5
  5.1 7.2 %all-gather = bf16[8,3,32,128]{3,2,1,0:T(8,128)(2,1)S(1)} all-gather(bf16[2,3,32,128]{3,2,1,0:T(8,128)(2,1)S(1)} %bitcast.14), channel_id=2, replica_groups=mesh['refl'=4,'atom'=32] {'refl'}, dimensions={0}, use_global_device_ids=true | all-gather | bytes 245760 | tf_op jit(solution)/shard_map/all_gather | solution.py:481
  12.3 0.0 collective-permute-done.halo_ref
  12.3 0.0 copy-done.1
  12.3 0.0 copy-done.3
  12.3 0.0 copy-done.4
  12.4 0.6 %copy-done.10 = bf16[3,128]{1,0:T(4,128)(2,1)S(1)} copy-done((bf16[3,128]{1,0:T(4,128)(2,1)S(1)}, bf16[3,128]{1,0:T(4,128)(2,1)}, u32[]{:S(2)}) %copy-start.10) | copy-done | bytes 792
  13.0 0.0 copy-done.6
  13.0 0.0 copy-done.9
  13.0 1.0 %copy-done = bf16[2048,128]{1,0:T(8,128)(2,1)S(1)} copy-done((bf16[2048,128]{1,0:T(8,128)(2,1)S(1)}, bf16[2048,128]{1,0:T(8,128)(2,1)}, u32[]{:S(2)}) %copy-start) | copy-done | bytes 524312
  14.1 9.6 %attend.1 = (bf16[2048,128]{1,0:T(8,128)(2,1)}, bf16[1024,128]{1,0:T(8,128)(2,1)S(1)}, f32[32,896]{1,0:T(8,128)S(1)}) custom-call(s32[3,4,3]{2,1,0:T(4,128)S(1)} %bitcast.8, f32[4,3]{1,0:T(4,128)S(1)} %copy-done.6, bf16[2048,128]{1,0:T(8,128)(2,1)S(1)} %copy-done, bf16[128,128]{1,0:T(8,128)(2,1)S(1)} %collective-permute-done.halo_ref, ...), custom_call_target="tpu_custom_call" | custom-call | tf_op jit(solution)/shard_map/attend/pallas_call | solution.py:494
  23.6 0.4 collective-permute-start.2
  24.0 1.0 %collective-permute-done.2.other_ref = f32[32,896]{1,0:T(8,128)S(1)} collective-permute-done((f32[32,896]{1,0:T(8,128)S(1)}, f32[32,896]{1,0:T(8,128)S(1)}, u32[]{:S(2)}, u32[]{:S(2)}) %collective-permute-start.2) | collective-permute-done | bytes 114720 | tf_op jit(solution)/shard_map/ppermute | solution.py:535
  25.0 2.0 %gather.1 = f32[32,24,128]{2,1,0:T(8,128)} custom-call(s32[1,32]{1,0:T(1,128)S(1)} %copy-done.11, f32[32,896]{1,0:T(8,128)S(1)} %get-tuple-element.10.own_ref, f32[32,896]{1,0:T(8,128)S(1)} %collective-permute-done.2.other_ref, s32[3,1024]{1,0:T(4,128)S(1)} %copy-done.2), custom_call_target="tpu_custom_call" | custom-call | tf_op jit(solution)/shard_map/gather/pallas_call | solution.py:527
  26.9 8.8 %all-to-all-start = ((f32[32,24,128]{2,1,0:T(8,128)}), f32[32,24,128]{2,1,0:T(8,128)S(1)}, u32[]{:S(2)}, u32[]{:S(2)}) async-start(f32[32,24,128]{2,1,0:T(8,128)} %gather.1), calls=%async_computation | async-start | bytes 786432 | tf_op jit(solution)/shard_map/all_to_all | solution.py:539
  35.7 0.0 copy-start.7
  35.8 0.1 collective-permute-start.1
  35.9 11.2 %all-to-all-done.recv_ref = f32[32,24,128]{2,1,0:T(8,128)S(1)} async-done(((f32[32,24,128]{2,1,0:T(8,128)}), f32[32,24,128]{2,1,0:T(8,128)S(1)}, u32[]{:S(2)}, u32[]{:S(2)}) %all-to-all-start) | async-done | bytes 393248 | tf_op jit(solution)/shard_map/all_to_all | solution.py:539
  47.1 4.7 %gradient.1 = (f32[8,128]{1,0:T(8,128)S(1)}, f32[3,2048]{1,0:T(4,128)S(1)}) custom-call(s32[3,4,3]{2,1,0:T(4,128)S(1)} %bitcast.9, f32[4,3]{1,0:T(4,128)S(1)} %copy-done.6, f32[32,24,128]{2,1,0:T(8,128)S(1)} %all-to-all-done.recv_ref, s32[3,1024]{1,0:T(4,128)S(1)} %copy-done.2, f32[8,128]{1,0:T(8,128)S(1)} %bitcast.11, f32[8,128]{1,0:T(8,128)S(1)} %bitcast.12), custom_call_target="tpu_custom_call" | custom-call | tf_op jit(solution)/shard_map/gradient/pallas_call | solution.py:540
  51.8 0.1 collective-permute-start.3
  51.9 1.2 %collective-permute-done.3 = f32[3,2048]{1,0:T(4,128)S(1)} collective-permute-done((f32[3,2048]{1,0:T(4,128)S(1)}, f32[3,2048]{1,0:T(4,128)S(1)}, u32[]{:S(2)}, u32[]{:S(2)}) %collective-permute-start.3) | collective-permute-done | bytes 24608 | tf_op jit(solution)/shard_map/ppermute | solution.py:558
  53.1 3.3 %collective-permute-start.4 = (f32[3,2048]{1,0:T(4,128)S(1)}, f32[3,2048]{1,0:T(4,128)S(1)}, u32[]{:S(2)}, u32[]{:S(2)}) collective-permute-start(f32[3,2048]{1,0:T(4,128)S(1)} %add.23), channel_id=1, source_target_pairs={{0,64},{64,0},{32,96},{96,32},{1,65},{65,1},{33,97},{97,33},{2,66}... | collective-permute-start | bytes 73736 | tf_op jit(solution)/shard_map/ppermute | solution.py:559
  56.3 0.0 collective-permute-done.1
  56.4 0.0 copy-start.14
  56.4 0.7 %dynamic_slice.7 = f32[32]{0:T(128)} dynamic-slice(f32[1024]{0:T(1024)S(1)} %bitcast.13, s32[]{:T(128)S(6)} %select_n.19), dynamic_slice_sizes={32} | dynamic-slice | bytes 260 | tf_op jit(solution)/shard_map/dynamic_slice | solution.py:561
  57.1 1.5 %collective-permute-done.4 = f32[3,2048]{1,0:T(4,128)S(1)} collective-permute-done((f32[3,2048]{1,0:T(4,128)S(1)}, f32[3,2048]{1,0:T(4,128)S(1)}, u32[]{:S(2)}, u32[]{:S(2)}) %collective-permute-start.4) | collective-permute-done | bytes 24608 | tf_op jit(solution)/shard_map/ppermute | solution.py:559
  58.6 0.6 %add.24 = f32[3,2048]{1,0:T(4,128)} add(f32[3,2048]{1,0:T(4,128)S(1)} %add.23, f32[3,2048]{1,0:T(4,128)S(1)} %collective-permute-done.4) | non-fusion elementwise | flops 6144 | bytes 73728 | tf_op jit(solution)/shard_map/add | solution.py:559
  (19 shorter events, 0.1 us)
Async XLA Ops:
  0.6 4.4 %copy-start.12 = (bf16[2,3,128,32]{2,3,1,0:T(8,128)(2,1)S(1)}, bf16[2,3,128,32]{2,3,1,0:T(8,128)(2,1)}, u32[]{:S(2)}) copy-start(bf16[2,3,128,32]{2,3,1,0:T(8,128)(2,1)} %param.15) | copy-start | bytes 147460
  1.4 10.9 %collective-permute-start = (bf16[128,128]{1,0:T(8,128)(2,1)S(1)}, bf16[128,128]{1,0:T(8,128)(2,1)S(1)}, u32[]{:S(2)}, u32[]{:S(2)}) collective-permute-start(bf16[128,128]{1,0:T(8,128)(2,1)S(1)} %constant_dynamic-slice_fusion), channel_id=1, source_target_pairs={{0,1},{1,2},{2,3},{3,4},{4,5},{5,6},{6,7},{7,8},{8,9},{9,10},{10,1... | collective-permute-start | bytes 98312 | tf_op jit(solution)/shard_map/ppermute | solution.py:480
  5.0 7.3 %copy-start.1 = (bf16[2,128,128]{2,1,0:T(8,128)(2,1)S(1)}, bf16[2,128,128]{2,1,0:T(8,128)(2,1)}, u32[]{:S(2)}) copy-start(bf16[2,128,128]{2,1,0:T(8,128)(2,1)} %wout_ref.1) | copy-start | bytes 196612
  5.0 7.3 %copy-start.3 = (f32[3,2048]{1,0:T(4,128)S(1)}, f32[3,2048]{1,0:T(4,128)}, u32[]{:S(2)}) copy-start(f32[3,2048]{1,0:T(4,128)} %noisy_ref.1) | copy-start | bytes 73732
  5.0 7.3 %copy-start.4 = (s32[4,3,3]{2,0,1:T(4,128)S(1)}, s32[4,3,3]{2,0,1:T(4,128)}, u32[]{:S(2)}) copy-start(s32[4,3,3]{2,0,1:T(4,128)} %param.22) | copy-start | bytes 436
  5.1 7.3 %copy-start.5 = (f32[2048]{0:T(1024)S(1)}, f32[2048]{0:T(1024)}, u32[]{:S(2)}) copy-start(f32[2048]{0:T(1024)} %param.19) | copy-start | bytes 24580
  12.3 0.7 %copy-start.10 = (bf16[3,128]{1,0:T(4,128)(2,1)S(1)}, bf16[3,128]{1,0:T(4,128)(2,1)}, u32[]{:S(2)}) copy-start(bf16[3,128]{1,0:T(4,128)(2,1)} %wcoord_ref.1) | copy-start | bytes 2308
  12.3 0.7 %copy-start.6 = (f32[4,3]{1,0:T(4,128)S(1)}, f32[4,3]{1,0:T(4,128)}, u32[]{:S(2)}) copy-start(f32[4,3]{1,0:T(4,128)} %shf_ref.3) | copy-start | bytes 148
  12.3 0.7 %copy-start.9 = (f32[2,128]{1,0:T(2,128)S(1)}, f32[2,128]{1,0:T(2,128)}, u32[]{:S(2)}) copy-start(f32[2,128]{1,0:T(2,128)} %gain_ref.1) | copy-start | bytes 3076
  13.0 1.0 %copy-start = (bf16[2048,128]{1,0:T(8,128)(2,1)S(1)}, bf16[2048,128]{1,0:T(8,128)(2,1)}, u32[]{:S(2)}) copy-start(bf16[2048,128]{1,0:T(8,128)(2,1)} %feat_ref.1) | copy-start | bytes 1572868
  14.1 10.9 %copy-start.2 = (s32[3,1024]{1,0:T(4,128)S(1)}, s32[3,1024]{1,0:T(4,128)}, u32[]{:S(2)}) copy-start(s32[3,1024]{1,0:T(4,128)} %miller_ref.3) | copy-start | bytes 36868
  23.6 1.3 %copy-start.11 = (s32[1,32]{1,0:T(1,128)S(1)}, s32[1,32]{1,0:T(1,128)}, u32[]{:S(2)}) copy-start(s32[1,32]{1,0:T(1,128)} %route_ref.1) | copy-start | bytes 388
  23.6 1.3 %collective-permute-start.2 = (f32[32,896]{1,0:T(8,128)S(1)}, f32[32,896]{1,0:T(8,128)S(1)}, u32[]{:S(2)}, u32[]{:S(2)}) collective-permute-start(f32[32,896]{1,0:T(8,128)S(1)} %get-tuple-element.10.own_ref), channel_id=1, source_target_pairs={{0,32},{32,0},{64,96},{96,64},{1,33},{33,1},{65,97},{97,65},{2,34}... | collective-permute-start | bytes 344072 | tf_op jit(solution)/shard_map/ppermute | solution.py:535
  26.9 20.2 %copy-start.8 = (f32[1024]{0:T(1024)S(1)}, f32[1024]{0:T(1024)}, u32[]{:S(2)}) copy-start(f32[1024]{0:T(1024)} %param.25) | copy-start | bytes 12292
  26.9 29.4 %copy-start.13 = (bf16[2048,128]{1,0:T(8,128)(2,1)S(1)}, bf16[2048,128]{1,0:T(8,128)(2,1)}, u32[]{:S(2)}) copy-start(bf16[2048,128]{1,0:T(8,128)(2,1)} %get-tuple-element.8) | copy-start | bytes 1572868
  26.9 20.1 %all-to-all-start = ((f32[32,24,128]{2,1,0:T(8,128)}), f32[32,24,128]{2,1,0:T(8,128)S(1)}, u32[]{:S(2)}, u32[]{:S(2)}) async-start(f32[32,24,128]{2,1,0:T(8,128)} %gather.1), calls=%async_computation | async-start | bytes 786432 | tf_op jit(solution)/shard_map/all_to_all | solution.py:539
  35.7 11.3 %copy-start.7 = (f32[1024]{0:T(1024)S(1)}, f32[1024]{0:T(1024)}, u32[]{:S(2)}) copy-start(f32[1024]{0:T(1024)} %param.24) | copy-start | bytes 12292
  35.8 20.6 %collective-permute-start.1 = (bf16[1024,128]{1,0:T(8,128)(2,1)S(1)}, bf16[1024,128]{1,0:T(8,128)(2,1)S(1)}, u32[]{:S(2)}, u32[]{:S(2)}) collective-permute-start(bf16[1024,128]{1,0:T(8,128)(2,1)S(1)} %get-tuple-element.9), channel_id=1, source_target_pairs={{0,32},{32,0},{64,96},{96,64},{1,33},{33,1},{65,97},{97,65},{2,34}... | collective-permute-start | bytes 786440 | tf_op jit(solution)/shard_map/ppermute | solution.py:537
  51.8 1.3 %collective-permute-start.3 = (f32[3,2048]{1,0:T(4,128)S(1)}, f32[3,2048]{1,0:T(4,128)S(1)}, u32[]{:S(2)}, u32[]{:S(2)}) collective-permute-start(f32[3,2048]{1,0:T(4,128)S(1)} %get-tuple-element.12), channel_id=1, source_target_pairs={{0,32},{32,0},{64,96},{96,64},{1,33},{33,1},{65,97},{97,65},{2,34}... | collective-permute-start | bytes 73736 | tf_op jit(solution)/shard_map/ppermute | solution.py:558
  53.1 5.5 %collective-permute-start.4 = (f32[3,2048]{1,0:T(4,128)S(1)}, f32[3,2048]{1,0:T(4,128)S(1)}, u32[]{:S(2)}, u32[]{:S(2)}) collective-permute-start(f32[3,2048]{1,0:T(4,128)S(1)} %add.23), channel_id=1, source_target_pairs={{0,64},{64,0},{32,96},{96,32},{1,65},{65,1},{33,97},{97,33},{2,66}... | collective-permute-start | bytes 73736 | tf_op jit(solution)/shard_map/ppermute | solution.py:559
  56.4 2.8 %copy-start.14 = (bf16[2048,128]{1,0:T(8,128)(2,1)}, bf16[2048,128]{1,0:T(8,128)(2,1)S(1)}, u32[]{:S(2)}) copy-start(bf16[2048,128]{1,0:T(8,128)(2,1)S(1)} %constant_dynamic-update-slice_fusion) | copy-start | bytes 1572868
